TPU v7x, 256 devices: a whole 4x4x8 slice. The times are simulated.
256 devices in a mesh: gx: 32 (over z_hi, x, core), gy: 4 (over y), row: 2 (over z_lo).
Axes of the slice: x: 4, y: 4, z: 8 (z_hi: 4, z_lo: 2; z = z_hi * 2 + z_lo), core: 2. Of those that a mesh axis runs over, the one named last changes fastest.
Arguments:
- concentrations: float32 [2, 512, 128, 256], P(None, 'gx', 'gy', 'row'), may hold values from 0 to 1
- diffusivity: float32 [512, 128, 256], P('gx', 'gy', 'row'), may hold values from 0.25 to 1
- weight_first: bfloat16 [512, 1024], replicated, may hold values from -0.25 to 0.25
- weight_middle: bfloat16 [1024, 1024], replicated, may hold values from -0.1875 to 0.1875
- weight_last: bfloat16 [1024, 512], replicated, may hold values from -0.1875 to 0.1875
Outputs:
- concentrations_out: float32 [2, 512, 128, 256], P(None, 'gx', 'gy', 'row')
- grad_first: float32 [512, 1024], P(('gx', 'gy', 'row'))
- grad_middle: float32 [1024, 1024], P(('gx', 'gy', 'row'))
- grad_last: float32 [1024, 512], P(('gx', 'gy', 'row'))
All inputs are finite; a program needn't handle non-finite values.
Results may differ from a plain program's by a relative error of at most 0.00035.
Values may be sent and summed in bfloat16 or wider, within the bound.
A program may use at most 128 MiB of HBM per device.

v0:
```python
import jax
import jax.numpy as jnp
from jax import lax
from jax.sharding import PartitionSpec as P

STEPS = 6
PATCH = 8


def extended(array, sides, width):
    for axis, dim in sides:
        size, length = (lax.axis_size(axis), array.shape[dim])
        up = [(i, (i + 1) % size) for i in range(size)]
        down = [(j, i) for i, j in up]
        last = lax.slice_in_dim(array, length - width, length, axis=dim)
        leading = lax.slice_in_dim(array, 0, width, axis=dim)
        before = lax.ppermute(last, axis, up)
        after = lax.ppermute(leading, axis, down)
        array = jnp.concatenate([before, array, after], axis=dim)
    return array


def shifted(block, axis, distance):
    devices = range(lax.axis_size(axis))
    route = [(i - distance, i) for i in devices if i - distance in devices]
    return lax.ppermute(block, axis, route)


def react(activator, inhibitor, diffusivity, lap_activator, lap_inhibitor, forcing):
    product = activator * inhibitor * inhibitor
    new_activator = activator + 0.1 * (
        diffusivity * lap_activator - product + 0.04 * (1.0 - activator) + forcing
    )
    new_inhibitor = inhibitor + 0.1 * (
        0.5 * diffusivity * lap_inhibitor + product - 0.1 * inhibitor
    )
    return (new_activator, new_inhibitor)


def advance(state, diffusivity, forcing):
    padded = extended(state, (("gx", 1), ("gy", 2), ("row", 3)), 1)
    center = padded[:, 1:-1, 1:-1, 1:-1]
    summed = -6.0 * center
    summed = summed + padded[:, 2:, 1:-1, 1:-1] + padded[:, :-2, 1:-1, 1:-1]
    summed = summed + padded[:, 1:-1, 2:, 1:-1] + padded[:, 1:-1, :-2, 1:-1]
    summed = summed + padded[:, 1:-1, 1:-1, 2:] + padded[:, 1:-1, 1:-1, :-2]
    new_activator, new_inhibitor = react(
        center[0], center[1], diffusivity, summed[0], summed[1], forcing
    )
    return jnp.stack([new_activator, new_inhibitor])


def to_patches(values, edge):
    extent_x, extent_y, extent_z = values.shape
    pieces = values.reshape(extent_x // edge, edge, extent_y // edge, edge, extent_z // edge, edge)
    return pieces.transpose(0, 2, 4, 1, 3, 5).reshape(-1, edge * edge * edge)


def from_patches(rows, shape, edge):
    extent_x, extent_y, extent_z = shape
    pieces = rows.reshape(extent_x // edge, extent_y // edge, extent_z // edge, edge, edge, edge)
    return pieces.transpose(0, 3, 1, 4, 2, 5).reshape(extent_x, extent_y, extent_z)


def gelu_back(pre_values, cotangent):
    unused, puller = jax.vjp(jax.nn.gelu, pre_values)
    return puller(cotangent)[0]


def learner(inputs, targets, weight_first, weight_middle, weight_last, scale):
    contract_rows = (((0,), (0,)), ((), ()))
    contract_cols = (((1,), (1,)), ((), ()))
    pre_first = jnp.dot(inputs, weight_first, preferred_element_type=jnp.float32)
    hidden_first = jax.nn.gelu(pre_first).astype(jnp.bfloat16)
    pre_second = jnp.dot(hidden_first, weight_middle, preferred_element_type=jnp.float32)
    hidden_second = jax.nn.gelu(pre_second).astype(jnp.bfloat16)
    forcing = jnp.dot(hidden_second, weight_last, preferred_element_type=jnp.float32)
    error = ((forcing - targets.astype(jnp.float32)) * scale).astype(jnp.bfloat16)
    grad_last = lax.dot_general(
        hidden_second, error, contract_rows, preferred_element_type=jnp.float32
    )
    carried = lax.dot_general(error, weight_last, contract_cols, preferred_element_type=jnp.float32)
    back_second = gelu_back(pre_second, carried).astype(jnp.bfloat16)
    grad_middle = lax.dot_general(
        hidden_first, back_second, contract_rows, preferred_element_type=jnp.float32
    )
    carried = lax.dot_general(
        back_second, weight_middle, contract_cols, preferred_element_type=jnp.float32
    )
    back_first = gelu_back(pre_first, carried).astype(jnp.bfloat16)
    grad_first = lax.dot_general(
        inputs, back_first, contract_rows, preferred_element_type=jnp.float32
    )
    return (forcing, grad_first, grad_middle, grad_last)


def per_device(concentrations, diffusivity, weight_first, weight_middle, weight_last):
    state = concentrations
    zero_force = jnp.zeros(state.shape[1:], jnp.float32)
    for repeat in range(STEPS // 2):
        state = advance(state, diffusivity, zero_force)
    inputs = to_patches(state[0], PATCH).astype(jnp.bfloat16)
    targets = to_patches(state[1], PATCH).astype(jnp.bfloat16)
    count = inputs.shape[0]
    scale = 1.0 / count
    stacked = jnp.stack([inputs, targets])
    arrived = shifted(stacked, "row", 1)
    batch_inputs = jnp.concatenate([arrived[0], inputs])
    batch_targets = jnp.concatenate([arrived[1], targets])
    is_learner = lax.axis_index("row") == 1

    def working(operands):
        return learner(operands[0], operands[1], weight_first, weight_middle, weight_last, scale)

    def resting(operands):
        return (
            jnp.zeros((2 * count, inputs.shape[1]), jnp.float32),
            jnp.zeros(weight_first.shape, jnp.float32),
            jnp.zeros(weight_middle.shape, jnp.float32),
            jnp.zeros(weight_last.shape, jnp.float32),
        )

    batch_forcing, grad_first, grad_middle, grad_last = lax.cond(
        is_learner, working, resting, (batch_inputs, batch_targets)
    )
    returned = shifted(batch_forcing[:count].astype(jnp.bfloat16), "row", -1).astype(jnp.float32)
    forcing_rows = jnp.where(is_learner, batch_forcing[count:], returned)
    grads = (
        lax.psum_scatter(grad_first, ("gx", "gy", "row"), scatter_dimension=0, tiled=True),
        lax.psum_scatter(grad_middle, ("gx", "gy", "row"), scatter_dimension=0, tiled=True),
        lax.psum_scatter(grad_last, ("gx", "gy", "row"), scatter_dimension=0, tiled=True),
    )
    forcing_field = from_patches(forcing_rows, state.shape[1:], PATCH)
    for repeat in range(STEPS - STEPS // 2):
        state = advance(state, diffusivity, forcing_field)
    return (state, grads[0], grads[1], grads[2])


def solution(mesh):
    in_specs = (P(None, "gx", "gy", "row"), P("gx", "gy", "row"), P(), P(), P())
    out_specs = (
        P(None, "gx", "gy", "row"),
        P(("gx", "gy", "row"), None),
        P(("gx", "gy", "row"), None),
        P(("gx", "gy", "row"), None),
    )
    return jax.shard_map(
        per_device, mesh=mesh, in_specs=in_specs, out_specs=out_specs, check_vma=False
    )
```

profile of v0, /device:TPU:8, one launch (start us, length us, event | category | flops | bytes accessed | tf_op | source)
XLA Modules:
  0.0 406.3 jit_solution(12778029114907426164)
XLA Ops:
  8.0 8.0 %collective-permute-start = (f32[2,1,32,128]{3,2,1,0:T(8,128)S(1)}, f32[2,1,32,128]{3,2,1,0:T(8,128)S(1)}, u32[]{:S(2)}, u32[]{:S(2)}) collective-permute-start(f32[2,1,32,128]{3,2,1,0:T(8,128)S(1)} %get-tuple-element.96), channel_id=1, source_target_pairs={{8,0},{16,8},{24,16},{32,24},{40,32},{48,40},{56,48},{64,56},{72,6... | collective-permute-start | bytes 98312 | tf_op jit(solution)/shard_map/ppermute | solution.py:18
  31.1 2.4 collective-permute-start.6
  35.1 6.0 %collective-permute-done.7 = f32[2,1,32,128]{3,2,1,0:T(8,128)S(1)} collective-permute-done((f32[2,1,32,128]{3,2,1,0:T(8,128)S(1)}, f32[2,1,32,128]{3,2,1,0:T(8,128)S(1)}, u32[]{:S(2)}, u32[]{:S(2)}) %collective-permute-start.7) | collective-permute-done | bytes 32800 | tf_op jit(solution)/shard_map/ppermute | solution.py:17
  41.1 3.0 collective-permute-start.8
  45.6 2.3 collective-permute-done.9
  57.0 6.0 %collective-permute-done.13 = f32[2,1,32,128]{3,2,1,0:T(8,128)S(1)} collective-permute-done((f32[2,1,32,128]{3,2,1,0:T(8,128)S(1)}, f32[2,1,32,128]{3,2,1,0:T(8,128)S(1)}, u32[]{:S(2)}, u32[]{:S(2)}) %collective-permute-start.13) | collective-permute-done | bytes 32800 | tf_op jit(solution)/shard_map/ppermute | solution.py:17
  75.4 3.4 convert_element_type.75
  78.7 3.1 copy.43
  82.5 3.4 convert_element_type.79
  85.9 3.1 copy.44
  89.7 3.0 collective-permute-start.24
  94.2 2.5 collective-permute-done.24
  97.4 4.7 %conditional.1 = (f32[256,512]{1,0:T(8,128)S(1)}, f32[512,1024]{0,1:T(8,128)S(1)}, f32[1024,1024]{1,0:T(8,128)}, f32[1024,512]{1,0:T(8,128)}) conditional(s32[]{:T(128)} %convert_element_type.73, () %tuple.16, (bf16[256,512]{0,1:T(8,128)(2,1)S(1)}, bf16[512,1024]{1,0:T(8,128)(2,1)}, bf16[1024,1024]{1,0:T(8,128)(2,1)}, bf16[1024,512]{1,0:T(8,128)(2,1)}, ...), branch_computations={%region_0.0_spmd, %region_1.0_spmd} | conditional | flops 2973761536 | bytes 64487792 | solution.py:123
  97.6 2.6 broadcast.34
  105.7 6.0 %collective-permute-done.19 = f32[2,1,32,128]{3,2,1,0:T(8,128)S(1)} collective-permute-done((f32[2,1,32,128]{3,2,1,0:T(8,128)S(1)}, f32[2,1,32,128]{3,2,1,0:T(8,128)S(1)}, u32[]{:S(2)}, u32[]{:S(2)}) %collective-permute-start.19) | collective-permute-done | bytes 32800 | tf_op jit(solution)/shard_map/ppermute | solution.py:17
  117.6 14.3 %collective-permute-start.22 = (f32[2,18,34,1]{2,0,3,1:T(2,128)S(1)}, f32[2,18,34,1]{2,0,3,1:T(2,128)S(1)}, u32[]{:S(2)}, u32[]{:S(2)}) collective-permute-start(f32[2,18,34,1]{2,0,3,1:T(2,128)S(1)} %copy.39), channel_id=1, source_target_pairs={{1,0},{0,1},{3,2},{2,3},{5,4},{4,5},{7,6},{6,7},{9,8},{8,9},{11,10... | collective-permute-start | bytes 14696 | tf_op jit(solution)/shard_map/ppermute | solution.py:18
  139.6 4.6 %collective-permute-done.25 = bf16[128,512]{1,0:T(8,128)(2,1)S(1)} collective-permute-done((bf16[128,512]{1,0:T(8,128)(2,1)S(1)}, bf16[128,512]{1,0:T(8,128)(2,1)S(1)}, u32[]{:S(2)}, u32[]{:S(2)}) %collective-permute-start.25) | collective-permute-done | bytes 131104 | tf_op jit(solution)/shard_map/ppermute | solution.py:26
  145.7 3.5 copy.50
  149.3 3.7 reshape.45
  154.9 6.3 %collective-permute-done.27 = f32[2,1,32,128]{3,2,1,0:T(8,128)S(1)} collective-permute-done((f32[2,1,32,128]{3,2,1,0:T(8,128)S(1)}, f32[2,1,32,128]{3,2,1,0:T(8,128)S(1)}, u32[]{:S(2)}, u32[]{:S(2)}) %collective-permute-start.27) | collective-permute-done | bytes 32800 | tf_op jit(solution)/shard_map/ppermute | solution.py:17
  167.7 2.1 collective-permute-start.31
  174.4 6.3 %collective-permute-done.33 = f32[2,1,32,128]{3,2,1,0:T(8,128)S(1)} collective-permute-done((f32[2,1,32,128]{3,2,1,0:T(8,128)S(1)}, f32[2,1,32,128]{3,2,1,0:T(8,128)S(1)}, u32[]{:S(2)}, u32[]{:S(2)}) %collective-permute-start.33) | collective-permute-done | bytes 32800 | tf_op jit(solution)/shard_map/ppermute | solution.py:17
  187.2 2.2 collective-permute-start.36
  195.6 199.6 %all-reduce.6.cloned.1.call-done = (f32[512,1024]{1,0:T(8,128)}, f32[1024,1024]{1,0:T(8,128)}, f32[1024,512]{1,0:T(8,128)}) async-done(((f32[512,1024]{1,0:T(8,128)}, f32[1024,1024]{1,0:T(8,128)}, f32[1024,512]{1,0:T(8,128)}), (f32[512,1024]{1,0:T(8,128)}, f32[1024,1024]{1,0:T(8,128)}, f32[1024,512]{1,0:T(8,128)})) %all-reduce.6.cloned.1.call-update) | async-done | bytes 8388624
  (151 shorter events, 94.0 us)
Async XLA Ops:
  7.2 388.0 %all-reduce.6.cloned.1.call-start = ((), (), s32[]{:S(2)}) async-start(), calls=%async_computation | async-start | bytes 16777216
  8.0 9.5 %collective-permute-start.1 = (f32[2,1,32,128]{3,2,1,0:T(8,128)S(1)}, f32[2,1,32,128]{3,2,1,0:T(8,128)S(1)}, u32[]{:S(2)}, u32[]{:S(2)}) collective-permute-start(f32[2,1,32,128]{3,2,1,0:T(8,128)S(1)} %get-tuple-element.97), channel_id=1, source_target_pairs={{0,8},{8,16},{16,24},{24,32},{32,40},{40,48},{48,56},{56,64},{64,7... | collective-permute-start | bytes 98312 | tf_op jit(solution)/shard_map/ppermute | solution.py:17
  8.0 10.6 %collective-permute-start = (f32[2,1,32,128]{3,2,1,0:T(8,128)S(1)}, f32[2,1,32,128]{3,2,1,0:T(8,128)S(1)}, u32[]{:S(2)}, u32[]{:S(2)}) collective-permute-start(f32[2,1,32,128]{3,2,1,0:T(8,128)S(1)} %get-tuple-element.96), channel_id=1, source_target_pairs={{8,0},{16,8},{24,16},{32,24},{40,32},{48,40},{56,48},{64,56},{72,6... | collective-permute-start | bytes 98312 | tf_op jit(solution)/shard_map/ppermute | solution.py:18
  18.7 3.8 collective-permute-start.2
  19.2 4.8 %collective-permute-start.3 = (f32[2,18,1,128]{3,2,1,0:T(1,128)S(1)}, f32[2,18,1,128]{3,2,1,0:T(1,128)S(1)}, u32[]{:S(2)}, u32[]{:S(2)}) collective-permute-start(f32[2,18,1,128]{3,2,1,0:T(1,128)S(1)} %get-tuple-element.84), channel_id=1, source_target_pairs={{0,2},{2,4},{4,6},{6,0},{1,3},{3,5},{5,7},{7,1},{8,10},{10,12},{12... | collective-permute-start | bytes 55304 | tf_op jit(solution)/shard_map/ppermute | solution.py:17
  31.1 4.0 collective-permute-start.6
  33.5 7.6 %collective-permute-start.7 = (f32[2,1,32,128]{3,2,1,0:T(8,128)S(1)}, f32[2,1,32,128]{3,2,1,0:T(8,128)S(1)}, u32[]{:S(2)}, u32[]{:S(2)}) collective-permute-start(f32[2,1,32,128]{3,2,1,0:T(8,128)S(1)} %get-tuple-element.94), channel_id=1, source_target_pairs={{0,8},{8,16},{16,24},{24,32},{32,40},{40,48},{48,56},{56,64},{64,7... | collective-permute-start | bytes 98312 | tf_op jit(solution)/shard_map/ppermute | solution.py:17
  41.1 4.5 %collective-permute-start.8 = (f32[2,18,1,128]{3,2,1,0:T(1,128)S(1)}, f32[2,18,1,128]{3,2,1,0:T(1,128)S(1)}, u32[]{:S(2)}, u32[]{:S(2)}) collective-permute-start(f32[2,18,1,128]{3,2,1,0:T(1,128)S(1)} %get-tuple-element.83), channel_id=1, source_target_pairs={{2,0},{4,2},{6,4},{0,6},{3,1},{5,3},{7,5},{1,7},{10,8},{12,10},{14... | collective-permute-start | bytes 55304 | tf_op jit(solution)/shard_map/ppermute | solution.py:18
  50.1 4.0 collective-permute-start.11
  55.4 7.6 %collective-permute-start.13 = (f32[2,1,32,128]{3,2,1,0:T(8,128)S(1)}, f32[2,1,32,128]{3,2,1,0:T(8,128)S(1)}, u32[]{:S(2)}, u32[]{:S(2)}) collective-permute-start(f32[2,1,32,128]{3,2,1,0:T(8,128)S(1)} %get-tuple-element.92), channel_id=1, source_target_pairs={{0,8},{8,16},{16,24},{24,32},{32,40},{40,48},{48,56},{56,64},{64,7... | collective-permute-start | bytes 98312 | tf_op jit(solution)/shard_map/ppermute | solution.py:17
  63.0 3.8 collective-permute-start.14
  89.7 6.9 %collective-permute-start.24 = (bf16[2,128,512]{1,2,0:T(8,128)(2,1)S(1)}, bf16[2,128,512]{1,2,0:T(8,128)(2,1)S(1)}, u32[]{:S(2)}, u32[]{:S(2)}) collective-permute-start(bf16[2,128,512]{1,2,0:T(8,128)(2,1)S(1)} %pad_maximum_fusion.142), channel_id=1, source_target_pairs={{0,1},{2,3},{4,5},{6,7},{8,9},{10,11},{12,13},{14,15},{16,17},{18,... | collective-permute-start | bytes 786440 | tf_op jit(solution)/shard_map/ppermute | solution.py:26
  104.1 7.6 %collective-permute-start.19 = (f32[2,1,32,128]{3,2,1,0:T(8,128)S(1)}, f32[2,1,32,128]{3,2,1,0:T(8,128)S(1)}, u32[]{:S(2)}, u32[]{:S(2)}) collective-permute-start(f32[2,1,32,128]{3,2,1,0:T(8,128)S(1)} %get-tuple-element.90), channel_id=1, source_target_pairs={{0,8},{8,16},{16,24},{24,32},{32,40},{40,48},{48,56},{56,64},{64,7... | collective-permute-start | bytes 98312 | tf_op jit(solution)/shard_map/ppermute | solution.py:17
  111.7 3.8 collective-permute-start.20
  117.6 16.3 %collective-permute-start.22 = (f32[2,18,34,1]{2,0,3,1:T(2,128)S(1)}, f32[2,18,34,1]{2,0,3,1:T(2,128)S(1)}, u32[]{:S(2)}, u32[]{:S(2)}) collective-permute-start(f32[2,18,34,1]{2,0,3,1:T(2,128)S(1)} %copy.39), channel_id=1, source_target_pairs={{1,0},{0,1},{3,2},{2,3},{5,4},{4,5},{7,6},{6,7},{9,8},{8,9},{11,10... | collective-permute-start | bytes 14696 | tf_op jit(solution)/shard_map/ppermute | solution.py:18
  132.2 3.9 collective-permute-start.23
  136.5 7.6 %collective-permute-start.25 = (bf16[128,512]{1,0:T(8,128)(2,1)S(1)}, bf16[128,512]{1,0:T(8,128)(2,1)S(1)}, u32[]{:S(2)}, u32[]{:S(2)}) collective-permute-start(bf16[128,512]{1,0:T(8,128)(2,1)S(1)} %slice.656), channel_id=1, source_target_pairs={{1,0},{3,2},{5,4},{7,6},{9,8},{11,10},{13,12},{15,14},{17,16},{19,... | collective-permute-start | bytes 393224 | tf_op jit(solution)/shard_map/ppermute | solution.py:26
  153.3 7.9 %collective-permute-start.27 = (f32[2,1,32,128]{3,2,1,0:T(8,128)S(1)}, f32[2,1,32,128]{3,2,1,0:T(8,128)S(1)}, u32[]{:S(2)}, u32[]{:S(2)}) collective-permute-start(f32[2,1,32,128]{3,2,1,0:T(8,128)S(1)} %get-tuple-element.88), channel_id=1, source_target_pairs={{0,8},{8,16},{16,24},{24,32},{32,40},{40,48},{48,56},{56,64},{64,7... | collective-permute-start | bytes 98312 | tf_op jit(solution)/shard_map/ppermute | solution.py:17
  161.3 3.8 collective-permute-start.28
  162.6 3.9 collective-permute-start.29
  167.7 3.9 collective-permute-start.31
  172.8 7.9 %collective-permute-start.33 = (f32[2,1,32,128]{3,2,1,0:T(8,128)S(1)}, f32[2,1,32,128]{3,2,1,0:T(8,128)S(1)}, u32[]{:S(2)}, u32[]{:S(2)}) collective-permute-start(f32[2,1,32,128]{3,2,1,0:T(8,128)S(1)} %get-tuple-element.86), channel_id=1, source_target_pairs={{0,8},{8,16},{16,24},{24,32},{32,40},{40,48},{48,56},{56,64},{64,7... | collective-permute-start | bytes 98312 | tf_op jit(solution)/shard_map/ppermute | solution.py:17
  182.6 3.9 collective-permute-start.35
  187.2 4.0 collective-permute-start.36
  (18 other events, 60.5 us)
Sparse Core Ops, SparseCore 0:
  104.1 291.0 all-reduce.5
where the time goes:
time: 415 us; the launch traced here: 406 us
  waiting for transfers between devices  280 us (67%)
  starting transfers between devices  56.8 us (14%)
  local copies, waits for them, and re-layouts  46.9 us (11%)
  between operations  14.6 us (4%)
  other arithmetic  7.64 us (2%)
    unnamed x2, waiting for transfers between devices  200 us
    ppermute x18, waiting for transfers between devices, extended(): before = lax.ppermute(last, axis, up)  49.5 us
    ppermute x18, starting transfers between devices, extended(): after = lax.ppermute(leading, axis, down)  40.5 us
    ppermute x18, waiting for transfers between devices, extended(): after = lax.ppermute(leading, axis, down)  23.9 us
    ppermute x18, starting transfers between devices, extended(): before = lax.ppermute(last, axis, up)  11.6 us
  transfers between devices with their start and end apart: 39, of which 38 were waited for; matrix products, arithmetic and copies ran while one was open for 6% of the time, Pallas kernels for 0%

commit v1 on v0

v1 whole, which is shorter than its diff:
```python
import jax
import jax.numpy as jnp
from jax import lax
from jax.experimental import pallas as pl
from jax.experimental.pallas import tpu as pltpu
from jax.sharding import PartitionSpec as P

STEPS = 6
F32 = jnp.float32
BF16 = jnp.bfloat16
MESH = pl.DeviceIdType.MESH
BLOCKS = 8
GELU_A = 0.7978845608028654
GELU_B = 0.044715


def place():
    gx, gy, row = lax.axis_index("gx"), lax.axis_index("gy"), lax.axis_index("row")
    return {"core": gx % 2, "x": (gx // 2) % 4, "y": gy, "z": (gx // 8) * 2 + row}


def device(at):
    return {
        "gx": (at["z"] // 2) * 8 + at["x"] * 2 + at["core"],
        "gy": at["y"],
        "row": at["z"] % 2,
    }


def moved(at, axis, distance):
    size = {"core": 2, "x": 4, "y": 4, "z": 8}[axis]
    return device({**at, axis: (at[axis] + distance) % size})


def gelu_pair(values):
    squared = values * values
    bent = jnp.tanh(GELU_A * (values + GELU_B * (values * squared)))
    half = 0.5 * (1.0 + bent)
    slope = half + (0.5 * values) * (1.0 - bent * bent) * (
        GELU_A + (3.0 * GELU_A * GELU_B) * squared
    )
    return values * half, slope


def rows_of(left, right):
    return lax.dot_general(left, right, (((1,), (0,)), ((), ())), preferred_element_type=F32)


def rows_of_t(left, right):
    return lax.dot_general(left, right, (((1,), (1,)), ((), ())), preferred_element_type=F32)


def kernel(
    conc, diff_in, wf_in, wm_in, wl_in,
    conc_out, gf_out, gm_out, gl_out,
    st, diff, ysend, zsend, hy, hz, tiles_u, tiles_v, turned, forced,
    wf, wm, wl, order, primed, inputs, targets, slope1, slope2, hidden,
    left, left_in, right, grad, recv1, sum1, recv2, pack, recv3, fin,
    load_sem, out_sem, halo_send, halo_recv, pair_send, pair_recv,
    send1, take1, send2, take2, send3, take3,
):
    at = place()
    gx, gy, row = lax.axis_index("gx"), lax.axis_index("gy"), lax.axis_index("row")
    mate = moved(at, "core", 1)
    core = at["core"]

    loads = [
        pltpu.make_async_copy(conc, st.at[0, :, pl.ds(1, 16)], load_sem.at[0]),
        pltpu.make_async_copy(diff_in, diff, load_sem.at[1]),
        pltpu.make_async_copy(wf_in, wf, load_sem.at[2]),
        pltpu.make_async_copy(wm_in, wm, load_sem.at[3]),
        pltpu.make_async_copy(wl_in, wl, load_sem.at[4]),
    ]
    for copy in loads:
        copy.start()

    barrier = pltpu.get_barrier_semaphore()
    peers = [{"gx": (gx + 1) % 32}, {"gx": (gx + 31) % 32}]
    peers += [moved(at, "x", d) for d in (1, 2, 3)]
    peers += [moved(at, "y", d) for d in (1, 2, 3)]
    peers += [moved(at, "z", d) for d in range(1, 8)]
    for peer in peers:
        pl.semaphore_signal(barrier, inc=1, device_id=peer, device_id_type=MESH)

    iota_y = lax.broadcasted_iota(jnp.int32, (32, 128), 0)
    iota_z = lax.broadcasted_iota(jnp.int32, (32, 128), 1)

    def face_rows(par, x, new, packed):
        for f in (0, 1):
            ysend[par, 0, f, pl.ds(x, 1), :] = new[f][0:1, :]
            ysend[par, 1, f, pl.ds(x, 1), :] = new[f][31:32, :]
            k = f * 16 + x
            packed = jnp.where(iota_z == k, pltpu.roll(new[f], k, 1), packed)
            packed = jnp.where(iota_z == k + 32, pltpu.roll(new[f], k + 33, 1), packed)
        return packed

    def halo_copies(par):
        plan = [
            (st.at[par, :, 1], st.at[par, :, 17], {"gx": (gx + 31) % 32}),
            (st.at[par, :, 16], st.at[par, :, 0], {"gx": (gx + 1) % 32}),
            (ysend.at[par, 0], hy.at[par, 1], {"gy": (gy + 3) % 4}),
            (ysend.at[par, 1], hy.at[par, 0], {"gy": (gy + 1) % 4}),
            (zsend.at[par], hz.at[par], {"row": 1 - row}),
        ]
        return [
            pltpu.make_async_remote_copy(
                src_ref=src, dst_ref=dst,
                send_sem=halo_send.at[par, i], recv_sem=halo_recv.at[par, i],
                device_id=who, device_id_type=MESH,
            )
            for i, (src, dst, who) in enumerate(plan)
        ]

    def step(number, force):
        par, nxt = number % 2, (number + 1) % 2
        for copy in halo_copies(par):
            copy.wait_recv()
        if number >= 1:
            for copy in halo_copies(nxt):
                copy.wait_send()
        last = number == STEPS - 1

        def body(x, packed):
            hzv = hz[par]
            laps, centers = [], []
            for f in (0, 1):
                c = st[par, f, x + 1]
                y_next = hy[par, 1, f, pl.ds(x, 1), :]
                y_prev = hy[par, 0, f, pl.ds(x, 1), :]
                k = f * 16 + x
                yp = jnp.where(iota_y == 31, y_next, pltpu.roll(c, 31, 0))
                ym = jnp.where(iota_y == 0, y_prev, pltpu.roll(c, 1, 0))
                zp = jnp.where(iota_z == 127, pltpu.roll(hzv, 127 - k, 1), pltpu.roll(c, 127, 1))
                zm = jnp.where(iota_z == 0, pltpu.roll(hzv, 96 - k, 1), pltpu.roll(c, 1, 1))
                lap = -6.0 * c + st[par, f, x + 2] + st[par, f, x] + yp + ym + zp + zm
                laps.append(lap)
                centers.append(c)
            u, v = centers
            d = diff[x]
            product = u * v * v
            inner = d * laps[0] - product + 0.04 * (1.0 - u)
            if force:
                base = (x // 8) * 256 + (x % 8) * 8
                inner = inner + jnp.concatenate(
                    [forced[pl.ds(pl.multiple_of(base + py * 64, 8), 8), :] for py in range(4)], axis=0
                )
            new_u = u + 0.1 * inner
            new_v = v + 0.1 * (0.5 * d * laps[1] + product - 0.1 * v)
            st[nxt, 0, x + 1] = new_u
            st[nxt, 1, x + 1] = new_v
            if number == STEPS // 2 - 1:
                base = (x // 8) * 256 + (x % 8) * 8
                for py in range(4):
                    here = pl.ds(pl.multiple_of(base + py * 64, 8), 8)
                    tiles_u[here, :] = new_u[py * 8:py * 8 + 8, :]
                    tiles_v[here, :] = new_v[py * 8:py * 8 + 8, :]
            if last:
                return packed
            return face_rows(nxt, x, (new_u, new_v), packed)

        packed = lax.fori_loop(0, 16, body, jnp.zeros((32, 128), F32))
        if not last:
            zsend[nxt] = packed
            for copy in halo_copies(nxt):
                copy.start()

    loads[0].wait()

    def first_faces(x, packed):
        return face_rows(0, x, (st[0, 0, x + 1], st[0, 1, x + 1]), packed)

    zsend[0] = lax.fori_loop(0, 16, first_faces, jnp.zeros((32, 128), F32))
    pl.semaphore_wait(barrier, len(peers))
    for copy in halo_copies(0):
        copy.start()

    r = lax.broadcasted_iota(jnp.int32, (512, 512), 0)
    c = lax.broadcasted_iota(jnp.int32, (512, 512), 1)
    order[0] = jnp.where(c == (r % 64) * 8 + r // 64, 1.0, 0.0).astype(BF16)
    for half in (0, 1):
        cell = (r // 128) * 128 + ((r // 32) % 4) * 32 + half * 16
        cell = cell + ((r // 8) % 4) * 4 + ((r // 4) % 2) * 2 + r % 2
        order[1 + half] = jnp.where(c == cell, 1.0, 0.0).astype(BF16)

    loads[1].wait()
    step(0, False)
    step(1, False)
    step(2, False)

    low = lax.broadcasted_iota(jnp.int32, (16, 128), 1) < 64
    for tiles, result in ((tiles_u, inputs), (tiles_v, targets)):
        for q in range(4):
            turned[q] = tiles[q * 128:q * 128 + 128, :].T
        for m in range(4):
            for q in range(4):
                a = turned[q, pl.ds(2 * m, 16, stride=8), :]
                b = turned[q, pl.ds(2 * m + 1, 16, stride=8), :]
                even = jnp.where(low, a, pltpu.roll(b, 64, 1))
                odd = jnp.where(low, pltpu.roll(a, 64, 1), b)
                primed[q * 32:q * 32 + 16, m * 128:m * 128 + 128] = even.astype(BF16)
                primed[q * 32 + 16:q * 32 + 32, m * 128:m * 128 + 128] = odd.astype(BF16)
        result[...] = rows_of(primed[...], order[0]).astype(BF16)

    def pair_copy(i):
        if i < 3:
            src = left_in.at[1 - core] if i == 0 else left.at[i - 1, 1 - core]
            dst = left_in.at[2] if i == 0 else left.at[i - 1, 2]
        else:
            cols = pl.ds(*((0, 1024), (1024, 1024), (2048, 512))[i - 3])
            src, dst = right.at[0, :, cols], right.at[1, :, cols]
        return pltpu.make_async_remote_copy(
            src_ref=src, dst_ref=dst, send_sem=pair_send.at[i], recv_sem=pair_recv.at[i],
            device_id=mate, device_id_type=MESH,
        )

    def layer(source, weights, slopes, which):
        def body(j, carry):
            cols = pl.ds(pl.multiple_of(j * 256, 256), 256)
            value, slope = gelu_pair(rows_of(source[...], weights[:, cols]))
            slopes[:, cols] = slope
            hidden[which, :, cols] = value.astype(BF16)
            flipped = value.T.astype(BF16)
            for x in range(4):
                for half in (0, 1):
                    left[which, half, pl.ds(pl.multiple_of((j * 4 + x) * 32, 32), 32), :] = flipped[
                        x * 64 + half * 32:x * 64 + half * 32 + 32, :
                    ]
            return carry

        lax.fori_loop(0, 4, body, 0)

    loads[2].wait()
    layer(inputs, wf, slope1, 0)
    pair_copy(1).start()
    for half in (0, 1):
        left_in[half] = rows_of_t(order[1 + half], inputs[...]).astype(BF16)
    pair_copy(0).start()
    loads[3].wait()
    layer(hidden.at[0], wm, slope2, 1)
    pair_copy(2).start()
    loads[4].wait()
    forcing = rows_of(hidden[1], wl[...])
    right[0, :, 2048:2560] = ((forcing - targets[...].astype(F32)) * (1.0 / 128)).astype(BF16)
    pair_copy(5).start()

    top = forcing.astype(BF16)
    rest = forcing - top.astype(F32)
    middle = rest.astype(BF16)
    rest = (rest - middle.astype(F32)).astype(BF16)
    back = rows_of_t(top, order[0]) + rows_of_t(middle, order[0]) + rows_of_t(rest, order[0])
    for m in range(4):
        for q in range(4):
            even = back[q * 32:q * 32 + 16, m * 128:m * 128 + 128]
            odd = back[q * 32 + 16:q * 32 + 32, m * 128:m * 128 + 128]
            turned[q, pl.ds(2 * m, 16, stride=8), :] = jnp.where(low, even, pltpu.roll(odd, 64, 1))
            turned[q, pl.ds(2 * m + 1, 16, stride=8), :] = jnp.where(low, pltpu.roll(even, 64, 1), odd)
    for q in range(4):
        forced[q * 128:q * 128 + 128, :] = turned[q].T
    step(3, True)

    def backward(error_cols, weights, slopes, first_col):
        def body(j, carry):
            cols = pl.ds(pl.multiple_of(j * 256, 256), 256)
            carried = rows_of_t(right[0, :, error_cols], weights[cols, :])
            right[0, :, pl.ds(pl.multiple_of(first_col + j * 256, 256), 256)] = (
                carried * slopes[:, cols]
            ).astype(BF16)
            return carry

        lax.fori_loop(0, 4, body, 0)

    def stage(b, number, d):
        axis = "xy"[(b + number) % 2]
        if number == 0:
            src, dst, send, take = grad.at[b], recv1.at[b, d - 1], send1, take1
        else:
            src, dst, send, take = sum1.at[b], recv2.at[b, d - 1], send2, take2
        return pltpu.make_async_remote_copy(
            src_ref=src.at[(at[axis] + d) % 4], dst_ref=dst,
            send_sem=send.at[b, d - 1], recv_sem=take.at[b, d - 1],
            device_id=moved(at, axis, d), device_id_type=MESH,
        )

    def gradient(b, own, other, cols):
        both = jnp.concatenate([own, other], axis=1)
        columns = jnp.concatenate([right[0, :, cols], right[1, :, cols]], axis=0)
        return rows_of(both, columns)

    def keep(b, value):
        cut = value.reshape(4, 4, 4, 8, 256)
        for i in range(4):
            grad[b, i] = cut[:, i] if b % 2 == 0 else cut[:, :, i]
        for d in (1, 2, 3):
            stage(b, 0, d).start()

    backward(pl.ds(2048, 512), wl, slope2, 1024)
    pair_copy(4).start()
    pair_copy(2).wait_recv()
    pair_copy(5).wait_recv()
    for b in (0, 1):
        keep(b, gradient(b, left[1, core], left[1, 2], slice(2048 + b * 256, 2304 + b * 256)))
    backward(pl.ds(1024, 1024), wm, slope1, 0)
    pair_copy(3).start()
    pair_copy(1).wait_recv()
    pair_copy(4).wait_recv()
    for b in (2, 3, 4, 5):
        col = 1024 + (b - 2) * 256
        keep(b, gradient(b, left[0, core], left[0, 2], slice(col, col + 256)))
    pair_copy(0).wait_recv()
    pair_copy(3).wait_recv()
    upper = (lax.broadcasted_iota(jnp.int32, (512, 256), 0) // 2) % 2 == 0
    for b in (6, 7):
        col = (b - 6) * 256
        keep(
            b,
            jnp.where(
                upper,
                gradient(b, left_in[core], left_in[2], slice(col, col + 256)),
                gradient(b, left_in[core], left_in[2], slice(col + 512, col + 768)),
            ),
        )

    step(4, True)

    sub = lax.broadcasted_iota(jnp.int32, (8, 128), 0) < 4

    def after_first(b):
        axis = "xy"[b % 2]
        for d in (1, 2, 3):
            stage(b, 0, d).wait_recv()
        total = grad[b, at[axis]] + recv1[b, 0] + recv1[b, 1] + recv1[b, 2]
        for i in range(4):
            sum1[b, i] = total[:, i]
        for d in (1, 2, 3):
            stage(b, 1, d).start()

    def after_second(b):
        axis = "xy"[(b + 1) % 2]
        for d in (1, 2, 3):
            stage(b, 1, d).wait_recv()
        total = sum1[b, at[axis]] + recv2[b, 0] + recv2[b, 1] + recv2[b, 2]
        for zh in range(4):
            lo, hi = total[zh, :, :128], total[zh, :, 128:]
            here = slice(b * 128, b * 128 + 128)
            pack[2 * zh, :, here] = jnp.where(sub, lo, pltpu.roll(hi, 4, 0))
            pack[2 * zh + 1, :, here] = jnp.where(sub, pltpu.roll(lo, 4, 0), hi)

    def stage3(d):
        return pltpu.make_async_remote_copy(
            src_ref=pack.at[(at["z"] + d) % 8], dst_ref=recv3.at[d - 1],
            send_sem=send3.at[d - 1], recv_sem=take3.at[d - 1],
            device_id=moved(at, "z", d), device_id_type=MESH,
        )

    for b in range(BLOCKS):
        after_first(b)
    step(5, True)
    out = pltpu.make_async_copy(st.at[0, :, pl.ds(1, 16)], conc_out, out_sem)
    out.start()
    for b in range(BLOCKS):
        after_second(b)
    for d in range(1, 8):
        stage3(d).start()
    for d in range(1, 8):
        stage3(d).wait_recv()
    total = pack[at["z"]]
    for d in range(7):
        total = total + recv3[d]

    def wide(b):
        part = total[:, b * 128:b * 128 + 128]
        return jnp.concatenate([part[0:4], part[4:8]], axis=1)

    gl_out[...] = jnp.concatenate([wide(0), wide(1)], axis=1)
    gm_out[...] = jnp.concatenate([wide(b) for b in (2, 3, 4, 5)], axis=1)
    whole = jnp.concatenate([wide(6), wide(7)], axis=1)
    gf_out[...] = jnp.concatenate([whole[0:2], whole[2:4]], axis=1)

    out.wait()
    for i in range(6):
        pair_copy(i).wait_send()
    for b in range(BLOCKS):
        for d in (1, 2, 3):
            stage(b, 0, d).wait_send()
            stage(b, 1, d).wait_send()
    for d in range(1, 8):
        stage3(d).wait_send()
    for copy in halo_copies((STEPS - 1) % 2):
        copy.wait_send()


def per_device(concentrations, diffusivity, weight_first, weight_middle, weight_last):
    any_space = pl.BlockSpec(memory_space=pl.ANY)
    vmem = pl.BlockSpec(memory_space=pltpu.VMEM)
    dma = pltpu.SemaphoreType.DMA
    return pl.pallas_call(
        kernel,
        out_shape=(
            jax.ShapeDtypeStruct((2, 16, 32, 128), F32),
            jax.ShapeDtypeStruct((2, 1024), F32),
            jax.ShapeDtypeStruct((4, 1024), F32),
            jax.ShapeDtypeStruct((4, 512), F32),
        ),
        in_specs=[any_space] * 5,
        out_specs=(any_space, vmem, vmem, vmem),
        scratch_shapes=[
            pltpu.VMEM((2, 2, 18, 32, 128), F32),
            pltpu.VMEM((16, 32, 128), F32),
            pltpu.VMEM((2, 2, 2, 16, 128), F32),
            pltpu.VMEM((2, 32, 128), F32),
            pltpu.VMEM((2, 2, 2, 16, 128), F32),
            pltpu.VMEM((2, 32, 128), F32),
            pltpu.VMEM((512, 128), F32),
            pltpu.VMEM((512, 128), F32),
            pltpu.VMEM((4, 128, 128), F32),
            pltpu.VMEM((512, 128), F32),
            pltpu.VMEM((512, 1024), BF16),
            pltpu.VMEM((1024, 1024), BF16),
            pltpu.VMEM((1024, 512), BF16),
            pltpu.VMEM((3, 512, 512), BF16),
            pltpu.VMEM((128, 512), BF16),
            pltpu.VMEM((128, 512), BF16),
            pltpu.VMEM((128, 512), BF16),
            pltpu.VMEM((128, 1024), F32),
            pltpu.VMEM((128, 1024), F32),
            pltpu.VMEM((2, 128, 1024), BF16),
            pltpu.VMEM((2, 3, 512, 128), BF16),
            pltpu.VMEM((3, 512, 128), BF16),
            pltpu.VMEM((2, 128, 2560), BF16),
            pltpu.VMEM((BLOCKS, 4, 4, 4, 8, 256), F32),
            pltpu.VMEM((BLOCKS, 3, 4, 4, 8, 256), F32),
            pltpu.VMEM((BLOCKS, 4, 4, 8, 256), F32),
            pltpu.VMEM((BLOCKS, 3, 4, 8, 256), F32),
            pltpu.VMEM((8, 8, BLOCKS * 128), F32),
            pltpu.VMEM((7, 8, BLOCKS * 128), F32),
            pltpu.VMEM((8, BLOCKS * 128), F32),
            dma((5,)), dma, dma((2, 5)), dma((2, 5)), dma((6,)), dma((6,)),
            dma((BLOCKS, 3)), dma((BLOCKS, 3)), dma((BLOCKS, 3)), dma((BLOCKS, 3)),
            dma((7,)), dma((7,)),
        ],
        compiler_params=pltpu.CompilerParams(
            collective_id=0, has_side_effects=True, vmem_limit_bytes=56 << 20
        ),
        name="whole_step",
    )(concentrations, diffusivity, weight_first, weight_middle, weight_last)


def solution(mesh):
    in_specs = (P(None, "gx", "gy", "row"), P("gx", "gy", "row"), P(), P(), P())
    out_specs = (
        P(None, "gx", "gy", "row"),
        P(("gx", "gy", "row"), None),
        P(("gx", "gy", "row"), None),
        P(("gx", "gy", "row"), None),
    )
    return jax.shard_map(
        per_device, mesh=mesh, in_specs=in_specs, out_specs=out_specs, check_vma=False
    )
```

time: 415 us -> 87.8 us (0.21)
  the two profiles are of different devices: /device:TPU:8 before, /device:TPU:1 now
where the time goes in v1:
time: 87.8 us; the launch traced here: 87.5 us
  Pallas kernels  81.1 us (92%)
  local copies, waits for them, and re-layouts  5.78 us (7%)
    pallas_call x1, Pallas kernels, per_device(): pl.pallas_call(kernel, out_shape=(jax.ShapeDtypeStruct((2, 16, 32, 128),...  81.1 us
    unnamed x4, local copies, waits for them, and re-layouts  5.78 us

profile of v1, /device:TPU:1, one launch (start us, length us, event | category | flops | bytes accessed | tf_op | source)
XLA Modules:
  0.0 87.5 jit_solution(4208260127963833864)
XLA Ops:
  0.6 81.1 %whole_step.1 = (f32[2,16,32,128]{3,2,1,0:T(8,128)}, f32[2,1024]{1,0:T(2,128)}, f32[4,1024]{1,0:T(4,128)}, f32[4,512]{1,0:T(4,128)}) custom-call(f32[2,16,32,128]{3,2,1,0:T(8,128)} %conc.1, f32[16,32,128]{2,1,0:T(8,128)} %diff_in.1, bf16[512,1024]{1,0:T(8,128)(2,1)} %wf_in.1, bf16[1024,1024]{1,0:T(8,128)(2,1)} %wm_in.1, bf16[1024,512]{1,0:T(8,128)(2,1)} %wl_in.1), custom_call_target="tpu_custom_call" | custom-call | tf_op jit(solution)/shard_map/whole_step/pallas_call | solution.py:396
  81.7 1.9 %copy.13 = f32[2,16,32,128]{3,2,1,0:T(8,128)} copy(f32[2,16,32,128]{3,2,1,0:T(8,128)} %get-tuple-element.8) | data formatting | bytes 1048576
  83.6 1.3 %copy.14 = f32[2,1024]{1,0:T(2,128)} copy(f32[2,1024]{1,0:T(2,128)} %get-tuple-element.9) | data formatting | bytes 16384
  84.9 1.3 %copy.15 = f32[4,1024]{1,0:T(4,128)} copy(f32[4,1024]{1,0:T(4,128)} %get-tuple-element.10) | data formatting | bytes 32768
  86.2 1.3 %copy.16 = f32[4,512]{1,0:T(4,128)} copy(f32[4,512]{1,0:T(4,128)} %get-tuple-element.11) | data formatting | bytes 16384

commit v2 on v1

--- a/solution.py
+++ b/solution.py
@@ -52,10 +52,10 @@
 
 def kernel(
     conc, diff_in, wf_in, wm_in, wl_in,
-    conc_out, gf_out, gm_out, gl_out,
+    conc_out, sums_out,
     st, diff, ysend, zsend, hy, hz, tiles_u, tiles_v, turned, forced,
     wf, wm, wl, order, primed, inputs, targets, slope1, slope2, hidden,
-    left, left_in, right, grad, recv1, sum1, recv2, pack, recv3, fin,
+    left, left_in, right, grad, recv1, sum1, recv2, pack, recv3,
     load_sem, out_sem, halo_send, halo_recv, pair_send, pair_recv,
     send1, take1, send2, take2, send3, take3,
 ):
@@ -84,14 +84,14 @@
 
     iota_y = lax.broadcasted_iota(jnp.int32, (32, 128), 0)
     iota_z = lax.broadcasted_iota(jnp.int32, (32, 128), 1)
+    pair_z = iota_z // 2
 
     def face_rows(par, x, new, packed):
         for f in (0, 1):
             ysend[par, 0, f, pl.ds(x, 1), :] = new[f][0:1, :]
             ysend[par, 1, f, pl.ds(x, 1), :] = new[f][31:32, :]
             k = f * 16 + x
-            packed = jnp.where(iota_z == k, pltpu.roll(new[f], k, 1), packed)
-            packed = jnp.where(iota_z == k + 32, pltpu.roll(new[f], k + 33, 1), packed)
+            packed = jnp.where(pair_z == k, pltpu.roll(new[f], 2 * k + 1, 1), packed)
         return packed
 
     def halo_copies(par):
@@ -113,7 +113,7 @@
 
     def step(number, force):
         par, nxt = number % 2, (number + 1) % 2
-        for copy in halo_copies(par):
+        for copy in halo_copies(par)[2:]:
             copy.wait_recv()
         if number >= 1:
             for copy in halo_copies(nxt):
@@ -130,8 +130,9 @@
                 k = f * 16 + x
                 yp = jnp.where(iota_y == 31, y_next, pltpu.roll(c, 31, 0))
                 ym = jnp.where(iota_y == 0, y_prev, pltpu.roll(c, 1, 0))
-                zp = jnp.where(iota_z == 127, pltpu.roll(hzv, 127 - k, 1), pltpu.roll(c, 127, 1))
-                zm = jnp.where(iota_z == 0, pltpu.roll(hzv, 96 - k, 1), pltpu.roll(c, 1, 1))
+                edges = pltpu.roll(hzv, 127 - 2 * k, 1)
+                zp = pltpu.roll(jnp.where(iota_z == 0, edges, c), 127, 1)
+                zm = pltpu.roll(jnp.where(iota_z == 127, edges, c), 1, 1)
                 lap = -6.0 * c + st[par, f, x + 2] + st[par, f, x] + yp + ym + zp + zm
                 laps.append(lap)
                 centers.append(c)
@@ -158,7 +159,11 @@
                 return packed
             return face_rows(nxt, x, (new_u, new_v), packed)
 
-        packed = lax.fori_loop(0, 16, body, jnp.zeros((32, 128), F32))
+        packed = lax.fori_loop(2, 14, body, jnp.zeros((32, 128), F32), unroll=4)
+        for copy in halo_copies(par)[:2]:
+            copy.wait_recv()
+        for x in (0, 1, 14, 15):
+            packed = body(x, packed)
         if not last:
             zsend[nxt] = packed
             for copy in halo_copies(nxt):
@@ -169,7 +174,7 @@
     def first_faces(x, packed):
         return face_rows(0, x, (st[0, 0, x + 1], st[0, 1, x + 1]), packed)
 
-    zsend[0] = lax.fori_loop(0, 16, first_faces, jnp.zeros((32, 128), F32))
+    zsend[0] = lax.fori_loop(0, 16, first_faces, jnp.zeros((32, 128), F32), unroll=4)
     pl.semaphore_wait(barrier, len(peers))
     for copy in halo_copies(0):
         copy.start()
@@ -242,6 +247,48 @@
     forcing = rows_of(hidden[1], wl[...])
     right[0, :, 2048:2560] = ((forcing - targets[...].astype(F32)) * (1.0 / 128)).astype(BF16)
     pair_copy(5).start()
+
+    def backward(error_cols, weights, slopes, first_col):
+        def body(j, carry):
+            cols = pl.ds(pl.multiple_of(j * 256, 256), 256)
+            carried = rows_of_t(right[0, :, error_cols], weights[cols, :])
+            right[0, :, pl.ds(pl.multiple_of(first_col + j * 256, 256), 256)] = (
+                carried * slopes[:, cols]
+            ).astype(BF16)
+            return carry
+
+        lax.fori_loop(0, 4, body, 0)
+
+    def stage(b, number, d):
+        axis = "xy"[(b + number) % 2]
+        if number == 0:
+            src, dst, send, take = grad.at[b], recv1.at[b, d - 1], send1, take1
+        else:
+            src, dst, send, take = sum1.at[b], recv2.at[b, d - 1], send2, take2
+        return pltpu.make_async_remote_copy(
+            src_ref=src.at[(at[axis] + d) % 4], dst_ref=dst,
+            send_sem=send.at[b, d - 1], recv_sem=take.at[b, d - 1],
+            device_id=moved(at, axis, d), device_id_type=MESH,
+        )
+
+    def gradient(b, own, other, cols):
+        both = jnp.concatenate([own, other], axis=1)
+        columns = jnp.concatenate([right[0, :, cols], right[1, :, cols]], axis=0)
+        return rows_of(both, columns)
+
+    def keep(b, value):
+        cut = value.reshape(4, 4, 4, 8, 256)
+        for i in range(4):
+            grad[b, i] = cut[:, i] if b % 2 == 0 else cut[:, :, i]
+        for d in (1, 2, 3):
+            stage(b, 0, d).start()
+
+    backward(pl.ds(2048, 512), wl, slope2, 1024)
+    pair_copy(4).start()
+    pair_copy(2).wait_recv()
+    pair_copy(5).wait_recv()
+    for b in (0, 1):
+        keep(b, gradient(b, left[1, core], left[1, 2], slice(2048 + b * 256, 2304 + b * 256)))
 
     top = forcing.astype(BF16)
     rest = forcing - top.astype(F32)
@@ -258,47 +305,6 @@
         forced[q * 128:q * 128 + 128, :] = turned[q].T
     step(3, True)
 
-    def backward(error_cols, weights, slopes, first_col):
-        def body(j, carry):
-            cols = pl.ds(pl.multiple_of(j * 256, 256), 256)
-            carried = rows_of_t(right[0, :, error_cols], weights[cols, :])
-            right[0, :, pl.ds(pl.multiple_of(first_col + j * 256, 256), 256)] = (
-                carried * slopes[:, cols]
-            ).astype(BF16)
-            return carry
-
-        lax.fori_loop(0, 4, body, 0)
-
-    def stage(b, number, d):
-        axis = "xy"[(b + number) % 2]
-        if number == 0:
-            src, dst, send, take = grad.at[b], recv1.at[b, d - 1], send1, take1
-        else:
-            src, dst, send, take = sum1.at[b], recv2.at[b, d - 1], send2, take2
-        return pltpu.make_async_remote_copy(
-            src_ref=src.at[(at[axis] + d) % 4], dst_ref=dst,
-            send_sem=send.at[b, d - 1], recv_sem=take.at[b, d - 1],
-            device_id=moved(at, axis, d), device_id_type=MESH,
-        )
-
-    def gradient(b, own, other, cols):
-        both = jnp.concatenate([own, other], axis=1)
-        columns = jnp.concatenate([right[0, :, cols], right[1, :, cols]], axis=0)
-        return rows_of(both, columns)
-
-    def keep(b, value):
-        cut = value.reshape(4, 4, 4, 8, 256)
-        for i in range(4):
-            grad[b, i] = cut[:, i] if b % 2 == 0 else cut[:, :, i]
-        for d in (1, 2, 3):
-            stage(b, 0, d).start()
-
-    backward(pl.ds(2048, 512), wl, slope2, 1024)
-    pair_copy(4).start()
-    pair_copy(2).wait_recv()
-    pair_copy(5).wait_recv()
-    for b in (0, 1):
-        keep(b, gradient(b, left[1, core], left[1, 2], slice(2048 + b * 256, 2304 + b * 256)))
     backward(pl.ds(1024, 1024), wm, slope1, 0)
     pair_copy(3).start()
     pair_copy(1).wait_recv()
@@ -341,14 +347,14 @@
         total = sum1[b, at[axis]] + recv2[b, 0] + recv2[b, 1] + recv2[b, 2]
         for zh in range(4):
             lo, hi = total[zh, :, :128], total[zh, :, 128:]
-            here = slice(b * 128, b * 128 + 128)
-            pack[2 * zh, :, here] = jnp.where(sub, lo, pltpu.roll(hi, 4, 0))
-            pack[2 * zh + 1, :, here] = jnp.where(sub, pltpu.roll(lo, 4, 0), hi)
-
-    def stage3(d):
+            here = slice(b % 2 * 128, b % 2 * 128 + 128)
+            pack[b // 2, 2 * zh, :, here] = jnp.where(sub, lo, pltpu.roll(hi, 4, 0))
+            pack[b // 2, 2 * zh + 1, :, here] = jnp.where(sub, pltpu.roll(lo, 4, 0), hi)
+
+    def stage3(piece, d):
         return pltpu.make_async_remote_copy(
-            src_ref=pack.at[(at["z"] + d) % 8], dst_ref=recv3.at[d - 1],
-            send_sem=send3.at[d - 1], recv_sem=take3.at[d - 1],
+            src_ref=pack.at[piece, (at["z"] + d) % 8], dst_ref=recv3.at[piece, d - 1],
+            send_sem=send3.at[piece, d - 1], recv_sem=take3.at[piece, d - 1],
             device_id=moved(at, "z", d), device_id_type=MESH,
         )
 
@@ -359,22 +365,16 @@
     out.start()
     for b in range(BLOCKS):
         after_second(b)
-    for d in range(1, 8):
-        stage3(d).start()
-    for d in range(1, 8):
-        stage3(d).wait_recv()
-    total = pack[at["z"]]
-    for d in range(7):
-        total = total + recv3[d]
-
-    def wide(b):
-        part = total[:, b * 128:b * 128 + 128]
-        return jnp.concatenate([part[0:4], part[4:8]], axis=1)
-
-    gl_out[...] = jnp.concatenate([wide(0), wide(1)], axis=1)
-    gm_out[...] = jnp.concatenate([wide(b) for b in (2, 3, 4, 5)], axis=1)
-    whole = jnp.concatenate([wide(6), wide(7)], axis=1)
-    gf_out[...] = jnp.concatenate([whole[0:2], whole[2:4]], axis=1)
+        if b % 2 == 1:
+            for d in range(1, 8):
+                stage3(b // 2, d).start()
+    for piece in range(4):
+        for d in range(1, 8):
+            stage3(piece, d).wait_recv()
+        total = pack[piece, at["z"]]
+        for d in range(7):
+            total = total + recv3[piece, d]
+        sums_out[:, piece * 256:piece * 256 + 256] = total
 
     out.wait()
     for i in range(6):
@@ -383,26 +383,48 @@
         for d in (1, 2, 3):
             stage(b, 0, d).wait_send()
             stage(b, 1, d).wait_send()
-    for d in range(1, 8):
-        stage3(d).wait_send()
+    for piece in range(4):
+        for d in range(1, 8):
+            stage3(piece, d).wait_send()
     for copy in halo_copies((STEPS - 1) % 2):
         copy.wait_send()
+
+
+def unpack(conc, sums, conc_out, gf_out, gm_out, gl_out, buffer, sem):
+    into, onward = [], []
+    for i in range(4):
+        here = (i // 2, pl.ds(i % 2 * 8, 8))
+        into.append(pltpu.make_async_copy(conc.at[here], buffer.at[here], sem.at[0, i]))
+        onward.append(pltpu.make_async_copy(buffer.at[here], conc_out.at[here], sem.at[1, i]))
+        into[-1].start()
+
+    def wide(b):
+        part = sums[:, b * 128:b * 128 + 128]
+        return jnp.concatenate([part[0:4], part[4:8]], axis=1)
+
+    gl_out[...] = jnp.concatenate([wide(0), wide(1)], axis=1)
+    gm_out[...] = jnp.concatenate([wide(b) for b in (2, 3, 4, 5)], axis=1)
+    whole = jnp.concatenate([wide(6), wide(7)], axis=1)
+    gf_out[...] = jnp.concatenate([whole[0:2], whole[2:4]], axis=1)
+    for i in range(4):
+        into[i].wait()
+        onward[i].start()
+    for copy in onward:
+        copy.wait()
 
 
 def per_device(concentrations, diffusivity, weight_first, weight_middle, weight_last):
     any_space = pl.BlockSpec(memory_space=pl.ANY)
     vmem = pl.BlockSpec(memory_space=pltpu.VMEM)
     dma = pltpu.SemaphoreType.DMA
-    return pl.pallas_call(
+    state, sums = pl.pallas_call(
         kernel,
         out_shape=(
             jax.ShapeDtypeStruct((2, 16, 32, 128), F32),
-            jax.ShapeDtypeStruct((2, 1024), F32),
-            jax.ShapeDtypeStruct((4, 1024), F32),
-            jax.ShapeDtypeStruct((4, 512), F32),
+            jax.ShapeDtypeStruct((8, BLOCKS * 128), F32),
         ),
         in_specs=[any_space] * 5,
-        out_specs=(any_space, vmem, vmem, vmem),
+        out_specs=(any_space, vmem),
         scratch_shapes=[
             pltpu.VMEM((2, 2, 18, 32, 128), F32),
             pltpu.VMEM((16, 32, 128), F32),
@@ -431,18 +453,30 @@
             pltpu.VMEM((BLOCKS, 3, 4, 4, 8, 256), F32),
             pltpu.VMEM((BLOCKS, 4, 4, 8, 256), F32),
             pltpu.VMEM((BLOCKS, 3, 4, 8, 256), F32),
-            pltpu.VMEM((8, 8, BLOCKS * 128), F32),
-            pltpu.VMEM((7, 8, BLOCKS * 128), F32),
-            pltpu.VMEM((8, BLOCKS * 128), F32),
+            pltpu.VMEM((4, 8, 8, 256), F32),
+            pltpu.VMEM((4, 7, 8, 256), F32),
             dma((5,)), dma, dma((2, 5)), dma((2, 5)), dma((6,)), dma((6,)),
             dma((BLOCKS, 3)), dma((BLOCKS, 3)), dma((BLOCKS, 3)), dma((BLOCKS, 3)),
-            dma((7,)), dma((7,)),
+            dma((4, 7)), dma((4, 7)),
         ],
         compiler_params=pltpu.CompilerParams(
             collective_id=0, has_side_effects=True, vmem_limit_bytes=56 << 20
         ),
         name="whole_step",
     )(concentrations, diffusivity, weight_first, weight_middle, weight_last)
+    return pl.pallas_call(
+        unpack,
+        out_shape=(
+            jax.ShapeDtypeStruct((2, 16, 32, 128), F32),
+            jax.ShapeDtypeStruct((2, 1024), F32),
+            jax.ShapeDtypeStruct((4, 1024), F32),
+            jax.ShapeDtypeStruct((4, 512), F32),
+        ),
+        in_specs=[any_space, vmem],
+        out_specs=(any_space, vmem, vmem, vmem),
+        scratch_shapes=[pltpu.VMEM((2, 16, 32, 128), F32), dma((2, 4))],
+        name="outputs",
+    )(state, sums)
 
 
 def solution(mesh):

time: 87.8 us -> 73.7 us (0.84)
  Pallas kernels: 81.1 us -> 72.9 us
  local copies, waits for them, and re-layouts: 5.78 us -> 0 us
    pallas_call x1, Pallas kernels: 81.1 us -> 69.8 us  [per_device(): pl.pallas_call(kernel, out_shape=(jax.ShapeDtypeStruct((2, 16, 32, 128),...]
    unnamed x4 -> x0, local copies, waits for them, and re-layouts: 5.78 us -> none
    pallas_call x0 -> x1, Pallas kernels: none -> 3.18 us  [per_device(): pl.pallas_call(unpack, out_shape=(jax.ShapeDtypeStruct((2, 16, 32, 128),...]
where the time goes in v2:
time: 73.7 us; the launch traced here: 73.6 us
  Pallas kernels  72.9 us (99%)
    pallas_call x1, Pallas kernels, per_device(): pl.pallas_call(kernel, out_shape=(jax.ShapeDtypeStruct((2, 16, 32, 128),...  69.8 us
    pallas_call x1, Pallas kernels, per_device(): pl.pallas_call(unpack, out_shape=(jax.ShapeDtypeStruct((2, 16, 32, 128),...  3.18 us

profile of v2, /device:TPU:1, one launch (start us, length us, event | category | flops | bytes accessed | tf_op | source)
XLA Modules:
  0.0 73.6 jit_solution(806011271818380258)
XLA Ops:
  0.6 69.8 %whole_step.1 = (f32[2,16,32,128]{3,2,1,0:T(8,128)}, f32[8,1024]{1,0:T(8,128)}) custom-call(f32[2,16,32,128]{3,2,1,0:T(8,128)} %conc.1, f32[16,32,128]{2,1,0:T(8,128)} %diff_in.1, bf16[512,1024]{1,0:T(8,128)(2,1)} %wf_in.1, bf16[1024,1024]{1,0:T(8,128)(2,1)} %wm_in.1, bf16[1024,512]{1,0:T(8,128)(2,1)} %wl_in.1), custom_call_target="tpu_custom_call" | custom-call | tf_op jit(solution)/shard_map/whole_step/pallas_call | solution.py:420
  70.4 3.2 %outputs.1 = (f32[2,16,32,128]{3,2,1,0:T(8,128)}, f32[2,1024]{1,0:T(2,128)}, f32[4,1024]{1,0:T(4,128)}, f32[4,512]{1,0:T(4,128)}) custom-call(f32[2,16,32,128]{3,2,1,0:T(8,128)} %get-tuple-element.6.conc, f32[8,1024]{1,0:T(8,128)} %get-tuple-element.7.sums), custom_call_target="tpu_custom_call" | custom-call | tf_op jit(solution)/shard_map/outputs/pallas_call | solution.py:467

commit v3 on v2

--- a/solution.py
+++ b/solution.py
@@ -10,6 +10,8 @@
 BF16 = jnp.bfloat16
 MESH = pl.DeviceIdType.MESH
 BLOCKS = 8
+HALVED = (1, 2)
+SLOT = {0: 0, 1: 1, 6: 2, 7: 3, 2: 0, 3: 1, 4: 2, 5: 3}
 GELU_A = 0.7978845608028654
 GELU_B = 0.044715
 
@@ -55,9 +57,10 @@
     conc_out, sums_out,
     st, diff, ysend, zsend, hy, hz, tiles_u, tiles_v, turned, forced,
     wf, wm, wl, order, primed, inputs, targets, slope1, slope2, hidden,
-    left, left_in, right, grad, recv1, sum1, recv2, pack, recv3,
+    left, left_in, right,
+    grad, recv1, sum1, recv2, pack, recv3, hgrad, hrecv, hrecv1, hsum1, hrecv2, hpack, hrecv3,
     load_sem, out_sem, halo_send, halo_recv, pair_send, pair_recv,
-    send1, take1, send2, take2, send3, take3,
+    half_send, half_take, send1, take1, send2, take2, send3, take3,
 ):
     at = place()
     gx, gy, row = lax.axis_index("gx"), lax.axis_index("gy"), lax.axis_index("row")
@@ -259,14 +262,26 @@
 
         lax.fori_loop(0, 4, body, 0)
 
+    def is_halved(b):
+        return b // 2 in HALVED
+
+    def halving(b):
+        distance = 1 + row * 6 if b % 2 == 0 else 7 - row * 6
+        return pltpu.make_async_remote_copy(
+            src_ref=hgrad.at[SLOT[b], 1 - row], dst_ref=hrecv.at[SLOT[b]],
+            send_sem=half_send.at[SLOT[b]], recv_sem=half_take.at[SLOT[b]],
+            device_id=moved(at, "z", distance), device_id_type=MESH,
+        )
+
     def stage(b, number, d):
-        axis = "xy"[(b + number) % 2]
-        if number == 0:
-            src, dst, send, take = grad.at[b], recv1.at[b, d - 1], send1, take1
+        axis, k = "xy"[(b + number) % 2], SLOT[b]
+        if is_halved(b):
+            src, dst = (hgrad.at[k, row], hrecv1) if number == 0 else (hsum1.at[k], hrecv2)
         else:
-            src, dst, send, take = sum1.at[b], recv2.at[b, d - 1], send2, take2
+            src, dst = (grad.at[k], recv1) if number == 0 else (sum1.at[k], recv2)
+        send, take = (send1, take1) if number == 0 else (send2, take2)
         return pltpu.make_async_remote_copy(
-            src_ref=src.at[(at[axis] + d) % 4], dst_ref=dst,
+            src_ref=src.at[(at[axis] + d) % 4], dst_ref=dst.at[k, d - 1],
             send_sem=send.at[b, d - 1], recv_sem=take.at[b, d - 1],
             device_id=moved(at, axis, d), device_id_type=MESH,
         )
@@ -276,12 +291,26 @@
         columns = jnp.concatenate([right[0, :, cols], right[1, :, cols]], axis=0)
         return rows_of(both, columns)
 
+    upper_half = lax.broadcasted_iota(jnp.int32, (64, 8, 128), 1) < 4
+
     def keep(b, value):
-        cut = value.reshape(4, 4, 4, 8, 256)
-        for i in range(4):
-            grad[b, i] = cut[:, i] if b % 2 == 0 else cut[:, :, i]
-        for d in (1, 2, 3):
-            stage(b, 0, d).start()
+        tiles = value.reshape(64, 8, 256)
+        lo, hi = tiles[:, :, :128], tiles[:, :, 128:]
+        even = jnp.where(upper_half, lo, pltpu.roll(hi, 4, 1))
+        odd = jnp.where(upper_half, pltpu.roll(lo, 4, 1), hi)
+        for zl, part in ((0, even), (1, odd)):
+            part = part.reshape(4, 4, 4, 8, 128)
+            for i in range(4):
+                cut = part[:, i] if b % 2 == 0 else part[:, :, i]
+                if is_halved(b):
+                    hgrad[SLOT[b], zl, i] = cut
+                else:
+                    grad[SLOT[b], i, :, zl] = cut
+        if is_halved(b):
+            halving(b).start()
+        else:
+            for d in (1, 2, 3):
+                stage(b, 0, d).start()
 
     backward(pl.ds(2048, 512), wl, slope2, 1024)
     pair_copy(4).start()
@@ -289,6 +318,26 @@
     pair_copy(5).wait_recv()
     for b in (0, 1):
         keep(b, gradient(b, left[1, core], left[1, 2], slice(2048 + b * 256, 2304 + b * 256)))
+    pair_copy(1).wait_recv()
+    pair_copy(4).wait_recv()
+    for b in (2, 3, 4, 5):
+        col = 1024 + (b - 2) * 256
+        keep(b, gradient(b, left[0, core], left[0, 2], slice(col, col + 256)))
+    backward(pl.ds(1024, 1024), wm, slope1, 0)
+    pair_copy(3).start()
+    pair_copy(0).wait_recv()
+    pair_copy(3).wait_recv()
+    upper = (lax.broadcasted_iota(jnp.int32, (512, 256), 0) // 2) % 2 == 0
+    for b in (6, 7):
+        col = (b - 6) * 256
+        keep(
+            b,
+            jnp.where(
+                upper,
+                gradient(b, left_in[core], left_in[2], slice(col, col + 256)),
+                gradient(b, left_in[core], left_in[2], slice(col + 512, col + 768)),
+            ),
+        )
 
     top = forcing.astype(BF16)
     rest = forcing - top.astype(F32)
@@ -305,76 +354,93 @@
         forced[q * 128:q * 128 + 128, :] = turned[q].T
     step(3, True)
 
-    backward(pl.ds(1024, 1024), wm, slope1, 0)
-    pair_copy(3).start()
-    pair_copy(1).wait_recv()
-    pair_copy(4).wait_recv()
-    for b in (2, 3, 4, 5):
-        col = 1024 + (b - 2) * 256
-        keep(b, gradient(b, left[0, core], left[0, 2], slice(col, col + 256)))
-    pair_copy(0).wait_recv()
-    pair_copy(3).wait_recv()
-    upper = (lax.broadcasted_iota(jnp.int32, (512, 256), 0) // 2) % 2 == 0
-    for b in (6, 7):
-        col = (b - 6) * 256
-        keep(
-            b,
-            jnp.where(
-                upper,
-                gradient(b, left_in[core], left_in[2], slice(col, col + 256)),
-                gradient(b, left_in[core], left_in[2], slice(col + 512, col + 768)),
-            ),
-        )
-
-    step(4, True)
-
-    sub = lax.broadcasted_iota(jnp.int32, (8, 128), 0) < 4
+    def after_half(b):
+        halving(b).wait_recv()
+        hgrad[SLOT[b], row] = hgrad[SLOT[b], row] + hrecv[SLOT[b]]
+        for d in (1, 2, 3):
+            stage(b, 0, d).start()
 
     def after_first(b):
-        axis = "xy"[b % 2]
+        k, me = SLOT[b], at["xy"[b % 2]]
         for d in (1, 2, 3):
             stage(b, 0, d).wait_recv()
-        total = grad[b, at[axis]] + recv1[b, 0] + recv1[b, 1] + recv1[b, 2]
-        for i in range(4):
-            sum1[b, i] = total[:, i]
+        if is_halved(b):
+            total = hgrad[k, row, me] + hrecv1[k, 0] + hrecv1[k, 1] + hrecv1[k, 2]
+            for i in range(4):
+                hsum1[k, i] = total[:, i]
+        else:
+            total = grad[k, me] + recv1[k, 0] + recv1[k, 1] + recv1[k, 2]
+            for i in range(4):
+                sum1[k, i] = total[:, :, i]
         for d in (1, 2, 3):
             stage(b, 1, d).start()
 
     def after_second(b):
-        axis = "xy"[(b + 1) % 2]
+        k, me = SLOT[b], at["xy"[(b + 1) % 2]]
         for d in (1, 2, 3):
             stage(b, 1, d).wait_recv()
-        total = sum1[b, at[axis]] + recv2[b, 0] + recv2[b, 1] + recv2[b, 2]
-        for zh in range(4):
-            lo, hi = total[zh, :, :128], total[zh, :, 128:]
-            here = slice(b % 2 * 128, b % 2 * 128 + 128)
-            pack[b // 2, 2 * zh, :, here] = jnp.where(sub, lo, pltpu.roll(hi, 4, 0))
-            pack[b // 2, 2 * zh + 1, :, here] = jnp.where(sub, pltpu.roll(lo, 4, 0), hi)
+        here = slice(b % 2 * 128, b % 2 * 128 + 128)
+        if is_halved(b):
+            total = hsum1[k, me] + hrecv2[k, 0] + hrecv2[k, 1] + hrecv2[k, 2]
+            hpack[k // 2, :, :, here] = total
+        else:
+            total = sum1[k, me] + recv2[k, 0] + recv2[k, 1] + recv2[k, 2]
+            pack[k // 2, :, :, here] = total.reshape(8, 8, 128)
 
     def stage3(piece, d):
+        k = SLOT[2 * piece] // 2
+        if piece in HALVED:
+            src, dst = hpack.at[k, (at["z"] // 2 + d) % 4], hrecv3.at[k, d - 1]
+            who = moved(at, "z", 2 * d)
+        else:
+            src, dst = pack.at[k, (at["z"] + d) % 8], recv3.at[k, d - 1]
+            who = moved(at, "z", d)
         return pltpu.make_async_remote_copy(
-            src_ref=pack.at[piece, (at["z"] + d) % 8], dst_ref=recv3.at[piece, d - 1],
+            src_ref=src, dst_ref=dst,
             send_sem=send3.at[piece, d - 1], recv_sem=take3.at[piece, d - 1],
-            device_id=moved(at, "z", d), device_id_type=MESH,
+            device_id=who, device_id_type=MESH,
         )
 
-    for b in range(BLOCKS):
-        after_first(b)
+    def hops(piece):
+        return range(1, 4) if piece in HALVED else range(1, 8)
+
+    def last_stage(piece):
+        after_second(2 * piece)
+        after_second(2 * piece + 1)
+        for d in hops(piece):
+            stage3(piece, d).start()
+
+    def finish(piece):
+        for d in hops(piece):
+            stage3(piece, d).wait_recv()
+        k = SLOT[2 * piece] // 2
+        total = hpack[k, at["z"] // 2] if piece in HALVED else pack[k, at["z"]]
+        for d in hops(piece):
+            total = total + (hrecv3[k, d - 1] if piece in HALVED else recv3[k, d - 1])
+        sums_out[:, piece * 256:piece * 256 + 256] = total
+
+    after_half(2)
+    after_half(3)
+    after_first(0)
+    after_first(1)
+    after_half(4)
+    after_half(5)
+    after_first(6)
+    after_first(7)
+    step(4, True)
+    after_first(2)
+    after_first(3)
+    last_stage(0)
+    after_first(4)
+    after_first(5)
+    last_stage(3)
+    last_stage(1)
     step(5, True)
     out = pltpu.make_async_copy(st.at[0, :, pl.ds(1, 16)], conc_out, out_sem)
     out.start()
-    for b in range(BLOCKS):
-        after_second(b)
-        if b % 2 == 1:
-            for d in range(1, 8):
-                stage3(b // 2, d).start()
-    for piece in range(4):
-        for d in range(1, 8):
-            stage3(piece, d).wait_recv()
-        total = pack[piece, at["z"]]
-        for d in range(7):
-            total = total + recv3[piece, d]
-        sums_out[:, piece * 256:piece * 256 + 256] = total
+    last_stage(2)
+    for piece in (0, 3, 1, 2):
+        finish(piece)
 
     out.wait()
     for i in range(6):
@@ -384,8 +450,11 @@
             stage(b, 0, d).wait_send()
             stage(b, 1, d).wait_send()
     for piece in range(4):
-        for d in range(1, 8):
+        for d in hops(piece):
             stage3(piece, d).wait_send()
+    for b in range(BLOCKS):
+        if is_halved(b):
+            halving(b).wait_send()
     for copy in halo_copies((STEPS - 1) % 2):
         copy.wait_send()
 
@@ -449,13 +518,21 @@
             pltpu.VMEM((2, 3, 512, 128), BF16),
             pltpu.VMEM((3, 512, 128), BF16),
             pltpu.VMEM((2, 128, 2560), BF16),
-            pltpu.VMEM((BLOCKS, 4, 4, 4, 8, 256), F32),
-            pltpu.VMEM((BLOCKS, 3, 4, 4, 8, 256), F32),
-            pltpu.VMEM((BLOCKS, 4, 4, 8, 256), F32),
-            pltpu.VMEM((BLOCKS, 3, 4, 8, 256), F32),
-            pltpu.VMEM((4, 8, 8, 256), F32),
-            pltpu.VMEM((4, 7, 8, 256), F32),
+            pltpu.VMEM((4, 4, 4, 2, 4, 8, 128), F32),
+            pltpu.VMEM((4, 3, 4, 2, 4, 8, 128), F32),
+            pltpu.VMEM((4, 4, 4, 2, 8, 128), F32),
+            pltpu.VMEM((4, 3, 4, 2, 8, 128), F32),
+            pltpu.VMEM((2, 8, 8, 256), F32),
+            pltpu.VMEM((2, 7, 8, 256), F32),
+            pltpu.VMEM((4, 2, 4, 4, 4, 8, 128), F32),
+            pltpu.VMEM((4, 4, 4, 4, 8, 128), F32),
+            pltpu.VMEM((4, 3, 4, 4, 8, 128), F32),
+            pltpu.VMEM((4, 4, 4, 8, 128), F32),
+            pltpu.VMEM((4, 3, 4, 8, 128), F32),
+            pltpu.VMEM((2, 4, 8, 256), F32),
+            pltpu.VMEM((2, 3, 8, 256), F32),
             dma((5,)), dma, dma((2, 5)), dma((2, 5)), dma((6,)), dma((6,)),
+            dma((4,)), dma((4,)),
             dma((BLOCKS, 3)), dma((BLOCKS, 3)), dma((BLOCKS, 3)), dma((BLOCKS, 3)),
             dma((4, 7)), dma((4, 7)),
         ],

time: 73.7 us -> 67 us (0.909)
  Pallas kernels: 72.9 us -> 66.2 us
    pallas_call x1, Pallas kernels: 69.8 us -> 63 us  [per_device(): pl.pallas_call(kernel, out_shape=(jax.ShapeDtypeStruct((2, 16, 32, 128),...]
where the time goes in v3:
time: 67 us; the launch traced here: 66.8 us
  Pallas kernels  66.2 us (99%)
    pallas_call x1, Pallas kernels, per_device(): pl.pallas_call(kernel, out_shape=(jax.ShapeDtypeStruct((2, 16, 32, 128),...  63 us
    pallas_call x1, Pallas kernels, per_device(): pl.pallas_call(unpack, out_shape=(jax.ShapeDtypeStruct((2, 16, 32, 128),...  3.18 us

profile of v3, /device:TPU:1, one launch (start us, length us, event | category | flops | bytes accessed | tf_op | source)
XLA Modules:
  0.0 66.8 jit_solution(10625094597522922714)
XLA Ops:
  0.6 63.0 %whole_step.1 = (f32[2,16,32,128]{3,2,1,0:T(8,128)}, f32[8,1024]{1,0:T(8,128)}) custom-call(f32[2,16,32,128]{3,2,1,0:T(8,128)} %conc.1, f32[16,32,128]{2,1,0:T(8,128)} %diff_in.1, bf16[512,1024]{1,0:T(8,128)(2,1)} %wf_in.1, bf16[1024,1024]{1,0:T(8,128)(2,1)} %wm_in.1, bf16[1024,512]{1,0:T(8,128)(2,1)} %wl_in.1), custom_call_target="tpu_custom_call" | custom-call | tf_op jit(solution)/shard_map/whole_step/pallas_call | solution.py:489
  63.6 3.2 %outputs.1 = (f32[2,16,32,128]{3,2,1,0:T(8,128)}, f32[2,1024]{1,0:T(2,128)}, f32[4,1024]{1,0:T(4,128)}, f32[4,512]{1,0:T(4,128)}) custom-call(f32[2,16,32,128]{3,2,1,0:T(8,128)} %get-tuple-element.6.conc, f32[8,1024]{1,0:T(8,128)} %get-tuple-element.7.sums), custom_call_target="tpu_custom_call" | custom-call | tf_op jit(solution)/shard_map/outputs/pallas_call | solution.py:544

commit v4 on v3

--- a/solution.py
+++ b/solution.py
@@ -235,7 +235,7 @@
                     ]
             return carry
 
-        lax.fori_loop(0, 4, body, 0)
+        lax.fori_loop(0, 4, body, 0, unroll=4)
 
     loads[2].wait()
     layer(inputs, wf, slope1, 0)
@@ -260,7 +260,7 @@
             ).astype(BF16)
             return carry
 
-        lax.fori_loop(0, 4, body, 0)
+        lax.fori_loop(0, 4, body, 0, unroll=4)
 
     def is_halved(b):
         return b // 2 in HALVED
@@ -459,14 +459,7 @@
         copy.wait_send()
 
 
-def unpack(conc, sums, conc_out, gf_out, gm_out, gl_out, buffer, sem):
-    into, onward = [], []
-    for i in range(4):
-        here = (i // 2, pl.ds(i % 2 * 8, 8))
-        into.append(pltpu.make_async_copy(conc.at[here], buffer.at[here], sem.at[0, i]))
-        onward.append(pltpu.make_async_copy(buffer.at[here], conc_out.at[here], sem.at[1, i]))
-        into[-1].start()
-
+def unpack(sums, gf_out, gm_out, gl_out):
     def wide(b):
         part = sums[:, b * 128:b * 128 + 128]
         return jnp.concatenate([part[0:4], part[4:8]], axis=1)
@@ -475,11 +468,6 @@
     gm_out[...] = jnp.concatenate([wide(b) for b in (2, 3, 4, 5)], axis=1)
     whole = jnp.concatenate([wide(6), wide(7)], axis=1)
     gf_out[...] = jnp.concatenate([whole[0:2], whole[2:4]], axis=1)
-    for i in range(4):
-        into[i].wait()
-        onward[i].start()
-    for copy in onward:
-        copy.wait()
 
 
 def per_device(concentrations, diffusivity, weight_first, weight_middle, weight_last):
@@ -489,11 +477,11 @@
     state, sums = pl.pallas_call(
         kernel,
         out_shape=(
-            jax.ShapeDtypeStruct((2, 16, 32, 128), F32),
+            pltpu.VMEM((2, 16, 32, 128), F32),
             jax.ShapeDtypeStruct((8, BLOCKS * 128), F32),
         ),
         in_specs=[any_space] * 5,
-        out_specs=(any_space, vmem),
+        out_specs=(vmem, vmem),
         scratch_shapes=[
             pltpu.VMEM((2, 2, 18, 32, 128), F32),
             pltpu.VMEM((16, 32, 128), F32),
@@ -541,19 +529,18 @@
         ),
         name="whole_step",
     )(concentrations, diffusivity, weight_first, weight_middle, weight_last)
-    return pl.pallas_call(
+    grads = pl.pallas_call(
         unpack,
         out_shape=(
-            jax.ShapeDtypeStruct((2, 16, 32, 128), F32),
             jax.ShapeDtypeStruct((2, 1024), F32),
             jax.ShapeDtypeStruct((4, 1024), F32),
             jax.ShapeDtypeStruct((4, 512), F32),
         ),
-        in_specs=[any_space, vmem],
-        out_specs=(any_space, vmem, vmem, vmem),
-        scratch_shapes=[pltpu.VMEM((2, 16, 32, 128), F32), dma((2, 4))],
+        in_specs=[vmem],
+        out_specs=(vmem, vmem, vmem),
         name="outputs",
-    )(state, sums)
+    )(sums)
+    return (state, *grads)
 
 
 def solution(mesh):

time: 67 us -> 63.7 us (0.951)
  Pallas kernels: 66.2 us -> 62.1 us
  local copies, waits for them, and re-layouts: 0 us -> 0.8 us
    pallas_call x2, Pallas kernels: 66.2 us -> 62.1 us  [the longest x1 60.7 us: per_device(): pl.pallas_call(kernel, out_shape=(pltpu.VMEM((2, 16, 32, 128), F32), jax....]
    unnamed x0 -> x1, local copies, waits for them, and re-layouts: none -> 0.8 us
where the time goes in v4:
time: 63.7 us; the launch traced here: 63.5 us
  Pallas kernels  62.1 us (97%)
  local copies, waits for them, and re-layouts  0.8 us (1%)
  between operations  0.64 us (1%)
    pallas_call x1, Pallas kernels, per_device(): pl.pallas_call(kernel, out_shape=(pltpu.VMEM((2, 16, 32, 128), F32), jax....  60.7 us
    pallas_call x1, Pallas kernels, per_device(): pl.pallas_call(unpack, out_shape=(jax.ShapeDtypeStruct((2, 1024), F32), j...  1.37 us

profile of v4, /device:TPU:1, one launch (start us, length us, event | category | flops | bytes accessed | tf_op | source)
XLA Modules:
  0.0 63.5 jit_solution(3227884058792451232)
XLA Ops:
  0.6 60.7 %whole_step.1 = (f32[2,16,32,128]{3,2,1,0:T(8,128)S(1)}, f32[8,1024]{1,0:T(8,128)}) custom-call(f32[2,16,32,128]{3,2,1,0:T(8,128)} %conc.1, f32[16,32,128]{2,1,0:T(8,128)} %diff_in.1, bf16[512,1024]{1,0:T(8,128)(2,1)} %wf_in.1, bf16[1024,1024]{1,0:T(8,128)(2,1)} %wm_in.1, bf16[1024,512]{1,0:T(8,128)(2,1)} %wl_in.1), custom_call_target="tpu_custom_call" | custom-call | tf_op jit(solution)/shard_map/whole_step/pallas_call | solution.py:477
  61.4 0.8 %copy.10 = f32[2,16,32,128]{3,2,1,0:T(8,128)} copy(f32[2,16,32,128]{3,2,1,0:T(8,128)S(1)} %get-tuple-element.14) | data formatting | bytes 1048576
  62.2 1.4 %outputs.1 = (f32[2,1024]{1,0:T(2,128)}, f32[4,1024]{1,0:T(4,128)}, f32[4,512]{1,0:T(4,128)}) custom-call(f32[8,1024]{1,0:T(8,128)} %get-tuple-element.10.sums), custom_call_target="tpu_custom_call" | custom-call | tf_op jit(solution)/shard_map/outputs/pallas_call | solution.py:532

commit v5 on v4

--- a/solution.py
+++ b/solution.py
@@ -60,7 +60,7 @@
     left, left_in, right,
     grad, recv1, sum1, recv2, pack, recv3, hgrad, hrecv, hrecv1, hsum1, hrecv2, hpack, hrecv3,
     load_sem, out_sem, halo_send, halo_recv, pair_send, pair_recv,
-    half_send, half_take, send1, take1, send2, take2, send3, take3,
+    near, far, half_send, half_take, send1, take1, send2, take2, send3, take3,
 ):
     at = place()
     gx, gy, row = lax.axis_index("gx"), lax.axis_index("gy"), lax.axis_index("row")
@@ -81,7 +81,7 @@
     peers = [{"gx": (gx + 1) % 32}, {"gx": (gx + 31) % 32}]
     peers += [moved(at, "x", d) for d in (1, 2, 3)]
     peers += [moved(at, "y", d) for d in (1, 2, 3)]
-    peers += [moved(at, "z", d) for d in range(1, 8)]
+    peers += [moved(at, "z", d) for d in (1, 7)]
     for peer in peers:
         pl.semaphore_signal(barrier, inc=1, device_id=peer, device_id_type=MESH)
 
@@ -114,59 +114,82 @@
             for i, (src, dst, who) in enumerate(plan)
         ]
 
-    def step(number, force):
+    def step(number, force, meanwhile=lambda: None):
         par, nxt = number % 2, (number + 1) % 2
-        for copy in halo_copies(par)[2:]:
-            copy.wait_recv()
+        last = number == STEPS - 1
         if number >= 1:
             for copy in halo_copies(nxt):
                 copy.wait_send()
-        last = number == STEPS - 1
-
-        def body(x, packed):
-            hzv = hz[par]
+
+        def inner(x, above, below):
             laps, centers = [], []
             for f in (0, 1):
                 c = st[par, f, x + 1]
-                y_next = hy[par, 1, f, pl.ds(x, 1), :]
-                y_prev = hy[par, 0, f, pl.ds(x, 1), :]
-                k = f * 16 + x
-                yp = jnp.where(iota_y == 31, y_next, pltpu.roll(c, 31, 0))
-                ym = jnp.where(iota_y == 0, y_prev, pltpu.roll(c, 1, 0))
-                edges = pltpu.roll(hzv, 127 - 2 * k, 1)
-                zp = pltpu.roll(jnp.where(iota_z == 0, edges, c), 127, 1)
-                zm = pltpu.roll(jnp.where(iota_z == 127, edges, c), 1, 1)
-                lap = -6.0 * c + st[par, f, x + 2] + st[par, f, x] + yp + ym + zp + zm
+                yp = jnp.where(iota_y == 31, 0.0, pltpu.roll(c, 31, 0))
+                ym = jnp.where(iota_y == 0, 0.0, pltpu.roll(c, 1, 0))
+                zp = jnp.where(iota_z == 127, 0.0, pltpu.roll(c, 127, 1))
+                zm = jnp.where(iota_z == 0, 0.0, pltpu.roll(c, 1, 1))
+                lap = -6.0 * c + yp + ym + zp + zm
+                if above:
+                    lap = lap + st[par, f, x + 2]
+                if below:
+                    lap = lap + st[par, f, x]
                 laps.append(lap)
                 centers.append(c)
             u, v = centers
             d = diff[x]
             product = u * v * v
-            inner = d * laps[0] - product + 0.04 * (1.0 - u)
+            change = d * laps[0] - product + 0.04 * (1.0 - u)
             if force:
                 base = (x // 8) * 256 + (x % 8) * 8
-                inner = inner + jnp.concatenate(
+                change = change + jnp.concatenate(
                     [forced[pl.ds(pl.multiple_of(base + py * 64, 8), 8), :] for py in range(4)], axis=0
                 )
-            new_u = u + 0.1 * inner
-            new_v = v + 0.1 * (0.5 * d * laps[1] + product - 0.1 * v)
-            st[nxt, 0, x + 1] = new_u
-            st[nxt, 1, x + 1] = new_v
+            st[nxt, 0, x + 1] = u + 0.1 * change
+            st[nxt, 1, x + 1] = v + 0.1 * (0.5 * d * laps[1] + product - 0.1 * v)
+
+        def inner_body(x, carry):
+            inner(x, True, True)
+            return carry
+
+        lax.fori_loop(1, 15, inner_body, 0, unroll=7)
+        inner(0, True, False)
+        inner(15, False, True)
+        meanwhile()
+        for copy in halo_copies(par)[2:]:
+            copy.wait_recv()
+        faces = hz[par]
+        faces = jnp.where(iota_z % 2 == 0, pltpu.roll(faces, 127, 1), pltpu.roll(faces, 1, 1))
+        edge_z = (iota_z == 0) | (iota_z == 127)
+
+        def finish_plane(x, packed, above=False, below=False):
+            d = 0.1 * diff[x]
+            new = []
+            for f in (0, 1):
+                y_next = hy[par, 1, f, pl.ds(x, 1), :]
+                y_prev = hy[par, 0, f, pl.ds(x, 1), :]
+                halo = jnp.where(edge_z, pltpu.roll(faces, 127 - 2 * (f * 16 + x), 1), 0.0)
+                halo = halo + jnp.where(iota_y == 31, y_next, jnp.where(iota_y == 0, y_prev, 0.0))
+                if above:
+                    halo = halo + st[par, f, x + 2]
+                if below:
+                    halo = halo + st[par, f, x]
+                value = st[nxt, f, x + 1] + (d if f == 0 else 0.5 * d) * halo
+                st[nxt, f, x + 1] = value
+                new.append(value)
             if number == STEPS // 2 - 1:
                 base = (x // 8) * 256 + (x % 8) * 8
                 for py in range(4):
                     here = pl.ds(pl.multiple_of(base + py * 64, 8), 8)
-                    tiles_u[here, :] = new_u[py * 8:py * 8 + 8, :]
-                    tiles_v[here, :] = new_v[py * 8:py * 8 + 8, :]
-            if last:
-                return packed
-            return face_rows(nxt, x, (new_u, new_v), packed)
-
-        packed = lax.fori_loop(2, 14, body, jnp.zeros((32, 128), F32), unroll=4)
+                    tiles_u[here, :] = new[0][py * 8:py * 8 + 8, :]
+                    tiles_v[here, :] = new[1][py * 8:py * 8 + 8, :]
+            return packed if last else face_rows(nxt, x, new, packed)
+
+        packed = lax.fori_loop(1, 15, finish_plane, jnp.zeros((32, 128), F32), unroll=7)
         for copy in halo_copies(par)[:2]:
             copy.wait_recv()
-        for x in (0, 1, 14, 15):
-            packed = body(x, packed)
+        packed = finish_plane(0, packed, below=True)
+        packed = finish_plane(15, packed, above=True)
         if not last:
             zsend[nxt] = packed
             for copy in halo_copies(nxt):
@@ -179,20 +202,31 @@
 
     zsend[0] = lax.fori_loop(0, 16, first_faces, jnp.zeros((32, 128), F32), unroll=4)
     pl.semaphore_wait(barrier, len(peers))
+    for d in (1, 7):
+        pl.semaphore_signal(near, inc=1, device_id=moved(at, "z", d), device_id_type=MESH)
     for copy in halo_copies(0):
         copy.start()
 
-    r = lax.broadcasted_iota(jnp.int32, (512, 512), 0)
-    c = lax.broadcasted_iota(jnp.int32, (512, 512), 1)
-    order[0] = jnp.where(c == (r % 64) * 8 + r // 64, 1.0, 0.0).astype(BF16)
-    for half in (0, 1):
-        cell = (r // 128) * 128 + ((r // 32) % 4) * 32 + half * 16
-        cell = cell + ((r // 8) % 4) * 4 + ((r // 4) % 2) * 2 + r % 2
-        order[1 + half] = jnp.where(c == cell, 1.0, 0.0).astype(BF16)
+    def build_order():
+        r = lax.broadcasted_iota(jnp.int32, (512, 512), 0)
+        c = lax.broadcasted_iota(jnp.int32, (512, 512), 1)
+        order[0] = jnp.where(c == ((r & 63) << 3) + (r >> 6), 1.0, 0.0).astype(BF16)
+
+    def build_shares():
+        r = lax.broadcasted_iota(jnp.int32, (512, 512), 0)
+        c = lax.broadcasted_iota(jnp.int32, (512, 512), 1)
+        for half in (0, 1):
+            cell = ((r >> 7) << 7) + (((r >> 5) & 3) << 5) + half * 16
+            cell = cell + (((r >> 3) & 3) << 2) + (((r >> 2) & 1) << 1) + (r & 1)
+            order[1 + half] = jnp.where(c == cell, 1.0, 0.0).astype(BF16)
 
     loads[1].wait()
-    step(0, False)
-    step(1, False)
+    step(0, False, build_order)
+    pl.semaphore_wait(near, 2)
+    for d in (2, 6):
+        pl.semaphore_signal(far, inc=1, device_id=moved(at, "z", d), device_id_type=MESH)
+    step(1, False, build_shares)
+    pl.semaphore_wait(far, 2)
     step(2, False)
 
     low = lax.broadcasted_iota(jnp.int32, (16, 128), 1) < 64
@@ -520,6 +554,7 @@
             pltpu.VMEM((2, 4, 8, 256), F32),
             pltpu.VMEM((2, 3, 8, 256), F32),
             dma((5,)), dma, dma((2, 5)), dma((2, 5)), dma((6,)), dma((6,)),
+            pltpu.SemaphoreType.REGULAR, pltpu.SemaphoreType.REGULAR,
             dma((4,)), dma((4,)),
             dma((BLOCKS, 3)), dma((BLOCKS, 3)), dma((BLOCKS, 3)), dma((BLOCKS, 3)),
             dma((4, 7)), dma((4, 7)),

time: 63.7 us -> 62.9 us (0.987)
  Pallas kernels: 62.1 us -> 61.3 us
    pallas_call x1, Pallas kernels: 60.7 us -> 59.9 us  [per_device(): pl.pallas_call(kernel, out_shape=(pltpu.VMEM((2, 16, 32, 128), F32), jax....]
where the time goes in v5:
time: 62.9 us; the launch traced here: 62.7 us
  Pallas kernels  61.3 us (97%)
  local copies, waits for them, and re-layouts  0.8 us (1%)
  between operations  0.64 us (1%)
    pallas_call x1, Pallas kernels, per_device(): pl.pallas_call(kernel, out_shape=(pltpu.VMEM((2, 16, 32, 128), F32), jax....  59.9 us
    pallas_call x1, Pallas kernels, per_device(): pl.pallas_call(unpack, out_shape=(jax.ShapeDtypeStruct((2, 1024), F32), j...  1.37 us

profile of v5, /device:TPU:1, one launch (start us, length us, event | category | flops | bytes accessed | tf_op | source)
XLA Modules:
  0.0 62.7 jit_solution(4373108219969227910)
XLA Ops:
  0.6 59.9 %whole_step.1 = (f32[2,16,32,128]{3,2,1,0:T(8,128)S(1)}, f32[8,1024]{1,0:T(8,128)}) custom-call(f32[2,16,32,128]{3,2,1,0:T(8,128)} %conc.1, f32[16,32,128]{2,1,0:T(8,128)} %diff_in.1, bf16[512,1024]{1,0:T(8,128)(2,1)} %wf_in.1, bf16[1024,1024]{1,0:T(8,128)(2,1)} %wm_in.1, bf16[1024,512]{1,0:T(8,128)(2,1)} %wl_in.1), custom_call_target="tpu_custom_call" | custom-call | tf_op jit(solution)/shard_map/whole_step/pallas_call | solution.py:511
  60.6 0.8 %copy.10 = f32[2,16,32,128]{3,2,1,0:T(8,128)} copy(f32[2,16,32,128]{3,2,1,0:T(8,128)S(1)} %get-tuple-element.14) | data formatting | bytes 1048576
  61.3 1.4 %outputs.1 = (f32[2,1024]{1,0:T(2,128)}, f32[4,1024]{1,0:T(4,128)}, f32[4,512]{1,0:T(4,128)}) custom-call(f32[8,1024]{1,0:T(8,128)} %get-tuple-element.10.sums), custom_call_target="tpu_custom_call" | custom-call | tf_op jit(solution)/shard_map/outputs/pallas_call | solution.py:567

commit v6 on v5

--- a/solution.py
+++ b/solution.py
@@ -343,7 +343,7 @@
         if is_halved(b):
             halving(b).start()
         else:
-            for d in (1, 2, 3):
+            for d in (2, 1, 3):
                 stage(b, 0, d).start()
 
     backward(pl.ds(2048, 512), wl, slope2, 1024)
@@ -391,7 +391,7 @@
     def after_half(b):
         halving(b).wait_recv()
         hgrad[SLOT[b], row] = hgrad[SLOT[b], row] + hrecv[SLOT[b]]
-        for d in (1, 2, 3):
+        for d in (2, 1, 3):
             stage(b, 0, d).start()
 
     def after_first(b):
@@ -406,7 +406,7 @@
             total = grad[k, me] + recv1[k, 0] + recv1[k, 1] + recv1[k, 2]
             for i in range(4):
                 sum1[k, i] = total[:, :, i]
-        for d in (1, 2, 3):
+        for d in (2, 1, 3):
             stage(b, 1, d).start()
 
     def after_second(b):
@@ -441,7 +441,7 @@
     def last_stage(piece):
         after_second(2 * piece)
         after_second(2 * piece + 1)
-        for d in hops(piece):
+        for d in sorted(hops(piece), key=lambda d: -min(d, len(hops(piece)) + 1 - d)):
             stage3(piece, d).start()
 
     def finish(piece):
@@ -469,10 +469,10 @@
     after_first(5)
     last_stage(3)
     last_stage(1)
+    last_stage(2)
     step(5, True)
     out = pltpu.make_async_copy(st.at[0, :, pl.ds(1, 16)], conc_out, out_sem)
     out.start()
-    last_stage(2)
     for piece in (0, 3, 1, 2):
         finish(piece)
 

time: 62.9 us -> 62.1 us (0.987)
  Pallas kernels: 61.3 us -> 60.5 us
    pallas_call x1, Pallas kernels: 59.9 us -> 59.1 us  [per_device(): pl.pallas_call(kernel, out_shape=(pltpu.VMEM((2, 16, 32, 128), F32), jax....]
where the time goes in v6:
time: 62.1 us; the launch traced here: 62 us
  Pallas kernels  60.5 us (97%)
  local copies, waits for them, and re-layouts  0.8 us (1%)
  between operations  0.64 us (1%)
    pallas_call x1, Pallas kernels, per_device(): pl.pallas_call(kernel, out_shape=(pltpu.VMEM((2, 16, 32, 128), F32), jax....  59.1 us
    pallas_call x1, Pallas kernels, per_device(): pl.pallas_call(unpack, out_shape=(jax.ShapeDtypeStruct((2, 1024), F32), j...  1.37 us

profile of v6, /device:TPU:1, one launch (start us, length us, event | category | flops | bytes accessed | tf_op | source)
XLA Modules:
  0.0 62.0 jit_solution(11439128655816233394)
XLA Ops:
  0.6 59.1 %whole_step.1 = (f32[2,16,32,128]{3,2,1,0:T(8,128)S(1)}, f32[8,1024]{1,0:T(8,128)}) custom-call(f32[2,16,32,128]{3,2,1,0:T(8,128)} %conc.1, f32[16,32,128]{2,1,0:T(8,128)} %diff_in.1, bf16[512,1024]{1,0:T(8,128)(2,1)} %wf_in.1, bf16[1024,1024]{1,0:T(8,128)(2,1)} %wm_in.1, bf16[1024,512]{1,0:T(8,128)(2,1)} %wl_in.1), custom_call_target="tpu_custom_call" | custom-call | tf_op jit(solution)/shard_map/whole_step/pallas_call | solution.py:511
  59.8 0.8 %copy.10 = f32[2,16,32,128]{3,2,1,0:T(8,128)} copy(f32[2,16,32,128]{3,2,1,0:T(8,128)S(1)} %get-tuple-element.14) | data formatting | bytes 1048576
  60.6 1.4 %outputs.1 = (f32[2,1024]{1,0:T(2,128)}, f32[4,1024]{1,0:T(4,128)}, f32[4,512]{1,0:T(4,128)}) custom-call(f32[8,1024]{1,0:T(8,128)} %get-tuple-element.10.sums), custom_call_target="tpu_custom_call" | custom-call | tf_op jit(solution)/shard_map/outputs/pallas_call | solution.py:567
